TPU v7x, 128 devices: a whole 4x4x4 slice. The times are simulated.
128 devices in a mesh: grp: 8 (over y, core), row: 16 (over z, x).
Axes of the slice: x: 4, y: 4, z: 4, core: 2. Of those that a mesh axis runs over, the one named last changes fastest.
Arguments:
- grad: float32 [128, 2048, 512], P('grp', 'row')
- weight: bfloat16 [128, 2048, 512], P('grp', 'row'), may hold values from -0.125 to 0.125
- owner: int32 [128, 1], P('grp'), may hold values from 0 to 15; in each aligned block of 16 rows (0 to 15, 16 to 31, ...) at most 2 rows name the same one
- tokens: bfloat16 [6144, 2048], P('row'), may hold values from -6 to 6
- counts: int32 [16], P('row'), may hold values from 96 to 384, as said below
Outputs:
- new_weight: bfloat16 [128, 2048, 512], P('grp', 'row')
- mixed: bfloat16 [6144, 512], P('row', 'grp')
Inputs may be any that keep to these rules, and one draw needn't show every extreme that they name: Within each group's 16 consecutive matrices no owner is named more than 2 times, a bound that some block reaches. `counts`: some row index has all 384 rows live.
All inputs are finite; a program needn't handle non-finite values.
Results may differ from a plain program's by a relative error of at most 0.017.
Values may be sent and summed in bfloat16 or wider, within the bound.
No kernel may reach another device: no remote copies, remote signals or barrier semaphores. Data moves between devices by JAX's collectives and lax.ppermute only.
A program may use at most 128 MiB of HBM per device.

v0:
```python
import jax
import jax.numpy as jnp
from jax import lax
from jax.experimental import pallas as pl
from jax.experimental.pallas import tpu as pltpu
from jax.sharding import Mesh
from jax.sharding import PartitionSpec as P

ITERS = 5
coef_a = 3.4445
coef_b = -4.775
coef_c = 2.0315
step_size = 0.5

f32 = jnp.float32
bf16 = jnp.bfloat16


def orthogonalize(x_ref, o_ref):
    rows, width = x_ref.shape
    step = rows // 4
    scale = None
    for turn in range(ITERS):
        source = x_ref if turn == 0 else o_ref
        x = source[...]
        gram = lax.dot_general(x, x, (((0,), (0,)), ((), ())), preferred_element_type=f32)
        if turn == 0:
            diagonal = lax.broadcasted_iota(jnp.int32, gram.shape, 0) == lax.broadcasted_iota(
                jnp.int32, gram.shape, 1
            )
            norm2 = jnp.sum(
                jnp.sum(jnp.where(diagonal, gram, 0.0), axis=0, keepdims=True),
                axis=1,
                keepdims=True,
            )
            scale = 1.0 / (jnp.sqrt(norm2) + 1e-07)
            gram = jnp.where(norm2 < jnp.inf, gram * scale * scale, 0.0)
        g = gram.astype(bf16)
        square = jnp.dot(g, g, preferred_element_type=f32)
        poly = (coef_b * g.astype(f32) + coef_c * square).astype(bf16)
        for part in range(4):
            at = pl.ds(part * step, step)
            piece = source[at, :]
            fresh = coef_a * piece.astype(f32) + jnp.dot(piece, poly, preferred_element_type=f32)
            if turn == 0:
                fresh = fresh * scale
            o_ref[at, :] = fresh.astype(bf16)


def update(owner_ref, core_ref, weight_ref, ortho_ref, new_ref, keep_ref, send_ref, table):
    number, halves, rows, width = weight_ref.shape
    owners = keep_ref.shape[1]
    tiles = width // 128

    @pl.when(pl.program_id(0) == 0)
    def _():
        for r in range(owners):
            table[0, r] = -1
            table[1, r] = -1
        for e in range(number):
            o = owner_ref[e]
            seen = table[0, o] >= 0
            table[1, o] = jnp.where(seen, e, table[1, o])
            table[0, o] = jnp.where(seen, table[0, o], e)

    for e in range(number):
        new_ref[e] = (
            weight_ref[e].astype(f32) - step_size * ortho_ref[e].astype(f32)
        ).astype(bf16)

    low = lax.broadcasted_iota(jnp.int32, (rows, 128), 1) < 64
    first_core = core_ref[0] == 0
    for r in range(owners):
        one, two = table[0, r], table[1, r]
        total = jnp.where(one >= 0, new_ref[jnp.maximum(one, 0)].astype(f32), 0.0)
        total = total + jnp.where(two >= 0, new_ref[jnp.maximum(two, 0)].astype(f32), 0.0)
        for t in range(tiles):
            top = total[0, :, t * 128 : (t + 1) * 128]
            bottom = pltpu.roll(total[1, :, t * 128 : (t + 1) * 128], 64, 1)
            mine = low == first_core
            keep_ref[t, r] = jnp.where(mine, top, bottom).astype(bf16)
            send_ref[t, r] = jnp.where(mine, bottom, top).astype(bf16)


def project(count_ref, core_ref, tokens_ref, sums_ref, out_ref, held):
    planes, owners, rows, lanes = sums_ref.shape
    for r in range(owners):
        total = sums_ref[0, r].astype(f32)
        for y in range(1, planes):
            total = total + sums_ref[y, r].astype(f32)
        held[pl.ds(r * 2 * rows, rows), :] = total.astype(bf16)
        held[pl.ds(r * 2 * rows + rows, rows), :] = pltpu.roll(total, 64, 1).astype(bf16)
    full = jnp.dot(tokens_ref[...], held[...], preferred_element_type=f32)
    mine = jnp.where(core_ref[0] == 0, full, pltpu.roll(full, 64, 1))[:, :64]
    live = lax.broadcasted_iota(jnp.int32, mine.shape, 0) < count_ref[0]
    out_ref[...] = jnp.where(live, mine * 8 ** (-0.5), 0.0).astype(bf16)


def body(grad, weight, owner, tokens, counts):
    number, rows, width = grad.shape
    ranks = lax.axis_size("row")
    planes = lax.axis_size("y")
    core = lax.axis_index("core")[None]
    vmem = pl.BlockSpec(memory_space=pltpu.VMEM)
    smem = pl.BlockSpec(memory_space=pltpu.SMEM)
    params = pltpu.CompilerParams(vmem_limit_bytes=48 * 1024 * 1024)

    whole = lax.all_to_all(grad.astype(bf16), "row", split_axis=0, concat_axis=0, tiled=True)
    ortho = pl.pallas_call(
        orthogonalize,
        out_shape=jax.ShapeDtypeStruct((ranks * rows, width), bf16),
        in_specs=[vmem],
        out_specs=vmem,
        compiler_params=params,
        name="orthogonalize",
    )(whole.reshape(ranks * rows, width))
    back = lax.all_to_all(
        ortho.reshape(ranks, rows, width), "row", split_axis=0, concat_axis=0, tiled=True
    )

    half = rows // 2
    block = pl.BlockSpec((number, 2, 16, width), lambda i: (0, 0, i, 0))
    packed = pl.BlockSpec((planes, ranks, 16, 128), lambda i: (0, 0, i, 0))
    new, keep, send = pl.pallas_call(
        update,
        grid=(half // 16,),
        out_shape=(
            jax.ShapeDtypeStruct((number, 2, half, width), bf16),
            jax.ShapeDtypeStruct((planes, ranks, half, 128), bf16),
            jax.ShapeDtypeStruct((planes, ranks, half, 128), bf16),
        ),
        in_specs=[smem, smem, block, block],
        out_specs=(block, packed, packed),
        scratch_shapes=[pltpu.SMEM((2, ranks), jnp.int32)],
        compiler_params=params,
        name="update",
    )(
        owner[:, 0],
        core,
        weight.reshape(number, 2, half, width),
        back.reshape(number, 2, half, width),
    )
    other = lax.ppermute(send, "core", [(0, 1), (1, 0)])
    pair = (keep.astype(f32) + other.astype(f32)).astype(bf16)
    sums = lax.all_to_all(
        pair.reshape(planes * ranks, half, 128),
        ("y", "row"),
        split_axis=0,
        concat_axis=0,
        tiled=True,
    ).reshape(planes, ranks, half, 128)
    mixed = pl.pallas_call(
        project,
        out_shape=jax.ShapeDtypeStruct((tokens.shape[0], width // (2 * planes)), bf16),
        in_specs=[smem, smem, vmem, vmem],
        out_specs=vmem,
        scratch_shapes=[pltpu.VMEM((ranks * rows, 128), bf16)],
        compiler_params=params,
        name="project",
    )(counts, core, tokens, sums)
    return new.reshape(number, rows, width), mixed


def solution(mesh):
    devices = mesh.devices.reshape(mesh.shape["grp"] // 2, 2, mesh.shape["row"])
    inner = Mesh(devices, ("y", "core", "row"))
    group = ("y", "core")
    return jax.shard_map(
        body,
        mesh=inner,
        in_specs=(
            P(group, "row", None),
            P(group, "row", None),
            P(group, None),
            P("row", None),
            P("row"),
        ),
        out_specs=(P(group, "row", None), P("row", group)),
        check_vma=False,
    )
```

profile of v0, /device:TPU:1, one launch (start us, length us, event | category | flops | bytes accessed | tf_op | source)
XLA Modules:
  0.0 124.0 jit_solution(9344065222079033165)
XLA Ops:
  0.6 2.5 %convert_element_type.12 = bf16[16,128,512]{2,1,0:T(8,128)(2,1)S(1)} convert(f32[16,128,512]{2,1,0:T(8,128)} %param.5) | non-fusion elementwise | flops 1048576 | bytes 6291456 | tf_op jit(solution)/shard_map/convert_element_type | solution.py:108
  3.1 35.6 %all_to_all.15 = bf16[16,128,512]{2,1,0:T(8,128)(2,1)S(1)} all-to-all(bf16[16,128,512]{2,1,0:T(8,128)(2,1)S(1)} %convert_element_type.12), channel_id=1, replica_groups=mesh['y'=4,'core'=2,'row'=16] {'row'}, dimensions={0} | all-to-all | bytes 4194304 | tf_op jit(solution)/shard_map/all_to_all | solution.py:108
  38.7 14.8 %orthogonalize.1 = bf16[2048,512]{1,0:T(8,128)(2,1)} custom-call(bf16[2048,512]{1,0:T(8,128)(2,1)S(1)} %bitcast.9), custom_call_target="tpu_custom_call" | custom-call | tf_op jit(solution)/shard_map/orthogonalize/pallas_call | solution.py:109
  53.5 0.0 copy-start
  53.5 0.0 copy-start.2
  53.5 4.6 %all-to-all-start.1 = ((bf16[16,128,512]{2,1,0:T(8,128)(2,1)}), bf16[16,128,512]{2,1,0:T(8,128)(2,1)}, u32[]{:S(2)}, u32[]{:S(2)}) async-start(bf16[16,128,512]{2,1,0:T(8,128)(2,1)} %bitcast.4), calls=%async_computation.1 | async-start | bytes 4194304 | tf_op jit(solution)/shard_map/all_to_all | solution.py:117
  58.1 27.3 %all-to-all-done.1 = bf16[16,128,512]{2,1,0:T(8,128)(2,1)} async-done(((bf16[16,128,512]{2,1,0:T(8,128)(2,1)}), bf16[16,128,512]{2,1,0:T(8,128)(2,1)}, u32[]{:S(2)}, u32[]{:S(2)}) %all-to-all-start.1) | async-done | bytes 2097184 | tf_op jit(solution)/shard_map/all_to_all | solution.py:117
  85.4 0.0 copy-done
  85.4 0.0 copy-done.2
  85.4 4.8 %update.1 = (bf16[16,2,64,512]{3,2,1,0:T(8,128)(2,1)}, bf16[4,16,64,128]{3,2,1,0:T(8,128)(2,1)S(1)}, bf16[4,16,64,128]{3,2,1,0:T(8,128)(2,1)S(1)}) custom-call(s32[16]{0:T(128)S(1)} %bitcast.12, s32[1]{0:T(128)} %bitcast.1.core_ref, bf16[16,2,64,512]{3,2,1,0:T(8,128)(2,1)S(1)} %bitcast.11, bf16[16,2,64,512]{3,2,1,0:T(8,128)(2,1)} %bitcast.5.ortho_ref), custom_call_target="tpu_custom_call" | custom-call | tf_op jit(solution)/shard_map/update/pallas_call | solution.py:124
  90.2 4.3 %collective-permute-start = (bf16[4,16,64,128]{3,2,1,0:T(8,128)(2,1)S(1)}, bf16[4,16,64,128]{3,2,1,0:T(8,128)(2,1)S(1)}, u32[]{:S(2)}, u32[]{:S(2)}) collective-permute-start(bf16[4,16,64,128]{3,2,1,0:T(8,128)(2,1)S(1)} %get-tuple-element.7), channel_id=1, source_target_pairs={{0,16},{16,0},{1,17},{17,1},{2,18},{18,2},{3,19},{19,3},{4,20},{20... | collective-permute-start | bytes 3145736 | tf_op jit(solution)/shard_map/ppermute | solution.py:143
  94.5 2.3 %collective-permute-done = bf16[4,16,64,128]{3,2,1,0:T(8,128)(2,1)S(1)} collective-permute-done((bf16[4,16,64,128]{3,2,1,0:T(8,128)(2,1)S(1)}, bf16[4,16,64,128]{3,2,1,0:T(8,128)(2,1)S(1)}, u32[]{:S(2)}, u32[]{:S(2)}) %collective-permute-start) | collective-permute-done | bytes 1048608 | tf_op jit(solution)/shard_map/ppermute | solution.py:143
  96.8 0.0 copy-start.1
  96.8 1.4 %add_convert_fusion = bf16[4,16,64,128]{3,2,1,0:T(8,128)(2,1)} fusion(bf16[4,16,64,128]{3,2,1,0:T(8,128)(2,1)S(1)} %collective-permute-done, bf16[4,16,64,128]{3,2,1,0:T(8,128)(2,1)S(1)} %get-tuple-element.6), kind=kLoop, calls=%fused_computation | loop fusion | flops 2097152 | bytes 3145728 | tf_op jit(solution)/shard_map/convert_element_type | solution.py:144
  98.2 6.2 %all-to-all-start.2 = ((bf16[64,64,128]{2,1,0:T(8,128)(2,1)}), bf16[64,64,128]{2,1,0:T(8,128)(2,1)S(1)}, u32[]{:S(2)}, u32[]{:S(2)}) async-start(bf16[64,64,128]{2,1,0:T(8,128)(2,1)} %bitcast.13), calls=%async_computation.2 | async-start | bytes 2097152 | tf_op jit(solution)/shard_map/all_to_all | solution.py:145
  105.0 17.4 %all-to-all-done.2 = bf16[64,64,128]{2,1,0:T(8,128)(2,1)S(1)} async-done(((bf16[64,64,128]{2,1,0:T(8,128)(2,1)}), bf16[64,64,128]{2,1,0:T(8,128)(2,1)S(1)}, u32[]{:S(2)}, u32[]{:S(2)}) %all-to-all-start.2) | async-done | bytes 1048608 | tf_op jit(solution)/shard_map/all_to_all | solution.py:145
  122.5 0.0 copy-done.1
  122.5 0.8 project.1
  123.3 0.7 copy.7
Async XLA Ops:
  53.5 31.9 %copy-start = (bf16[16,128,512]{2,1,0:T(8,128)(2,1)S(1)}, bf16[16,128,512]{2,1,0:T(8,128)(2,1)}, u32[]{:S(2)}) copy-start(bf16[16,128,512]{2,1,0:T(8,128)(2,1)} %param.6) | copy-start | bytes 6291460
  53.5 31.9 %copy-start.2 = (s32[16,1]{0,1:T(1,128)S(1)}, s32[16,1]{0,1:T(1,128)}, u32[]{:S(2)}) copy-start(s32[16,1]{0,1:T(1,128)} %param.7) | copy-start | bytes 196
  53.5 31.8 %all-to-all-start.1 = ((bf16[16,128,512]{2,1,0:T(8,128)(2,1)}), bf16[16,128,512]{2,1,0:T(8,128)(2,1)}, u32[]{:S(2)}, u32[]{:S(2)}) async-start(bf16[16,128,512]{2,1,0:T(8,128)(2,1)} %bitcast.4), calls=%async_computation.1 | async-start | bytes 4194304 | tf_op jit(solution)/shard_map/all_to_all | solution.py:117
  90.2 6.6 %collective-permute-start = (bf16[4,16,64,128]{3,2,1,0:T(8,128)(2,1)S(1)}, bf16[4,16,64,128]{3,2,1,0:T(8,128)(2,1)S(1)}, u32[]{:S(2)}, u32[]{:S(2)}) collective-permute-start(bf16[4,16,64,128]{3,2,1,0:T(8,128)(2,1)S(1)} %get-tuple-element.7), channel_id=1, source_target_pairs={{0,16},{16,0},{1,17},{17,1},{2,18},{18,2},{3,19},{19,3},{4,20},{20... | collective-permute-start | bytes 3145736 | tf_op jit(solution)/shard_map/ppermute | solution.py:143
  96.8 25.7 %copy-start.1 = (bf16[384,2048]{1,0:T(8,128)(2,1)S(1)}, bf16[384,2048]{1,0:T(8,128)(2,1)}, u32[]{:S(2)}) copy-start(bf16[384,2048]{1,0:T(8,128)(2,1)} %tokens_ref.1) | copy-start | bytes 4718596
  98.2 24.3 %all-to-all-start.2 = ((bf16[64,64,128]{2,1,0:T(8,128)(2,1)}), bf16[64,64,128]{2,1,0:T(8,128)(2,1)S(1)}, u32[]{:S(2)}, u32[]{:S(2)}) async-start(bf16[64,64,128]{2,1,0:T(8,128)(2,1)} %bitcast.13), calls=%async_computation.2 | async-start | bytes 2097152 | tf_op jit(solution)/shard_map/all_to_all | solution.py:145
where the time goes:
time: 125 us; the launch traced here: 124 us
  waiting for transfers between devices  47 us (38%)
  blocking collectives  35.6 us (28%)
  Pallas kernels  20.4 us (16%)
  starting transfers between devices  15.1 us (12%)
  other arithmetic  3.87 us (3%)
  between operations  1.32 us (1%)
    all_to_all x1, blocking collectives, body(): lax.all_to_all(grad.astype(bf16), 'row', split_axis=0, concat_axis=0, til...  35.6 us
    all_to_all x1, waiting for transfers between devices, body(): lax.all_to_all(ortho.reshape(ranks, rows, width), 'row', split_axis=0, co...  27.3 us
    all_to_all x1, waiting for transfers between devices, body(): lax.all_to_all(pair.reshape(planes * ranks, half, 128), ('y', 'row'), spl...  17.4 us
    pallas_call x1, Pallas kernels, body(): pl.pallas_call(orthogonalize, out_shape=jax.ShapeDtypeStruct((ranks * row...  14.8 us
    all_to_all x1, starting transfers between devices, body(): lax.all_to_all(pair.reshape(planes * ranks, half, 128), ('y', 'row'), spl...  6.18 us
    pallas_call x1, Pallas kernels, body(): pl.pallas_call(update, grid=(half // 16,), out_shape=(jax.ShapeDtypeStruc...  4.83 us
    all_to_all x1, starting transfers between devices, body(): lax.all_to_all(ortho.reshape(ranks, rows, width), 'row', split_axis=0, co...  4.57 us
    ppermute x1, starting transfers between devices, body(): other = lax.ppermute(send, 'core', [(0, 1), (1, 0)])  4.3 us
  transfers between devices with their start and end apart: 3, of which 3 were waited for; matrix products, arithmetic and copies ran while one was open for 0% of the time, Pallas kernels for 0%

commit v1 on v0

v1 whole, which is shorter than its diff:
```python
import jax
import jax.numpy as jnp
from jax import lax
from jax.experimental import pallas as pl
from jax.experimental.pallas import tpu as pltpu
from jax.sharding import Mesh
from jax.sharding import PartitionSpec as P

ITERS = 5
coef_a = 3.4445
coef_b = -4.775
coef_c = 2.0315
step_size = 0.5

f32 = jnp.float32
bf16 = jnp.bfloat16


def orthogonalize(x_ref, out_ref, held, staged, sems):
    rows = x_ref.shape[0]
    copies = []
    step = rows // 4
    scale = None
    for turn in range(ITERS):
        source = x_ref if turn == 0 else held
        x = source[...]
        gram = lax.dot_general(x, x, (((0,), (0,)), ((), ())), preferred_element_type=f32)
        if turn == 0:
            diagonal = lax.broadcasted_iota(jnp.int32, gram.shape, 0) == lax.broadcasted_iota(
                jnp.int32, gram.shape, 1
            )
            norm2 = jnp.sum(
                jnp.sum(jnp.where(diagonal, gram, 0.0), axis=0, keepdims=True),
                axis=1,
                keepdims=True,
            )
            scale = 1.0 / (jnp.sqrt(norm2) + 1e-07)
            gram = jnp.where(norm2 < jnp.inf, gram * scale * scale, 0.0)
        g = gram.astype(bf16)
        square = jnp.dot(g, g, preferred_element_type=f32)
        poly = (coef_b * g.astype(f32) + coef_c * square).astype(bf16)
        for part in range(4):
            at = pl.ds(part * step, step)
            piece = source[at, :]
            fresh = coef_a * piece.astype(f32) + jnp.dot(piece, poly, preferred_element_type=f32)
            if turn == 0:
                fresh = fresh * scale
            fresh = fresh.astype(bf16)
            if turn < ITERS - 1:
                held[at, :] = fresh
                continue
            staged[at, :] = fresh
            copies.append(pltpu.make_async_copy(staged.at[at], out_ref.at[at], sems.at[part]))
            copies[-1].start()
    for copy in copies:
        copy.wait()


def combine(owner_ref, pair_ref, core_ref, mine_ref, theirs_ref, ortho_ref, *refs):
    sum_ref, pass_ref, staged, table, sems, pass_sem = refs
    number, halves, rows, width = ortho_ref.shape
    lanes = rows // 2
    tiles = width // 128
    core = core_ref[0]
    passing = pltpu.make_async_copy(ortho_ref.at[:, 1 - core], pass_ref, pass_sem)
    passing.start()
    for source, named in enumerate((owner_ref, pair_ref)):
        for r in range(number):
            table[2 * source, r] = -1
            table[2 * source + 1, r] = -1
        for e in range(number):
            o = named[e]
            seen = table[2 * source, o] >= 0
            table[2 * source + 1, o] = jnp.where(seen, e, table[2 * source + 1, o])
            table[2 * source, o] = jnp.where(seen, table[2 * source, o], e)

    low = lax.broadcasted_iota(jnp.int32, (lanes, 128), 1) < 64
    copies = []
    for r in range(number):
        total = 0.0
        for slot in range(4):
            e = table[slot, r]
            at = jnp.maximum(e, 0)
            old_ref, source = (mine_ref, core) if slot < 2 else (theirs_ref, 1 - core)
            new = old_ref[at].astype(f32) - step_size * ortho_ref[at, source].astype(f32)
            total = total + jnp.where(e >= 0, new, 0.0)
        for t in range(tiles):
            top = total[:lanes, t * 128 : (t + 1) * 128]
            bottom = pltpu.roll(total[lanes:, t * 128 : (t + 1) * 128], 64, 1)
            staged[r, 2 * t] = jnp.where(low, top, bottom).astype(bf16)
            staged[r, 2 * t + 1] = jnp.where(low, bottom, top).astype(bf16)
        if r % 4 == 3:
            ready = pl.ds(r - 3, 4)
            copies.append(
                pltpu.make_async_copy(staged.at[ready], sum_ref.at[ready], sems.at[r // 4])
            )
            copies[-1].start()
    for copy in copies:
        copy.wait()
    passing.wait()


def project(count_ref, core_ref, tokens_ref, sums_ref, out_ref, held):
    ranks, planes, halves, rows, _ = sums_ref.shape
    for r in range(ranks):
        for h in range(halves):
            first = (2 * r + h) * 2 * rows
            total = sums_ref[r, 0, h].astype(f32)
            for y in range(1, planes):
                total = total + sums_ref[r, y, h].astype(f32)
            held[first : first + rows, :] = total.astype(bf16)
            held[first + rows : first + 2 * rows, :] = pltpu.roll(total, 64, 1).astype(bf16)
    full = jnp.dot(tokens_ref[...], held[...], preferred_element_type=f32).T
    mine = jnp.where(core_ref[0] == 0, full[:64], full[64:])
    live = lax.broadcasted_iota(jnp.int32, mine.shape, 1) < count_ref[0]
    out_ref[...] = jnp.where(live, mine * 8 ** (-0.5), 0.0).astype(bf16)


def body(grad, weight, owner, tokens, counts):
    number, rows, width = grad.shape
    ranks = lax.axis_size("row")
    planes = lax.axis_size("y")
    half = rows // 2
    index = lax.axis_index("core")
    core = index[None]
    vmem = pl.BlockSpec(memory_space=pltpu.VMEM)
    smem = pl.BlockSpec(memory_space=pltpu.SMEM)
    hbm = pl.BlockSpec(memory_space=pltpu.HBM)
    params = pltpu.CompilerParams(vmem_limit_bytes=20 * 1024 * 1024)
    swap = [(0, 1), (1, 0)]

    def exchange(data, axes):
        return lax.all_to_all(data, axes, split_axis=0, concat_axis=0, tiled=True)

    whole = exchange(grad.astype(bf16), "row")

    named = owner[:, 0]
    pair_named = lax.ppermute(named, "core", swap)
    split = weight.reshape(number, 2, half, width)
    mine = lax.dynamic_index_in_dim(split, index, 1, keepdims=False)
    theirs = lax.ppermute(
        lax.dynamic_index_in_dim(split, 1 - index, 1, keepdims=False), "core", swap
    )
    ortho = pl.pallas_call(
        orthogonalize,
        out_shape=pltpu.HBM((ranks * rows, width), bf16),
        in_specs=[vmem],
        out_specs=hbm,
        scratch_shapes=[
            pltpu.VMEM((ranks * rows, width), bf16),
            pltpu.VMEM((ranks * rows, width), bf16),
            pltpu.SemaphoreType.DMA((4,)),
        ],
        compiler_params=params,
        name="orthogonalize",
    )(whole.reshape(ranks * rows, width))
    back = exchange(ortho.reshape(2 * ranks, half, width), ("row", "core"))
    back = back.reshape(number, 2, half, width)

    lanes = half // 2
    sums, passed = pl.pallas_call(
        combine,
        out_shape=(
            pltpu.HBM((ranks, 2 * planes, lanes, 128), bf16),
            pltpu.HBM((number, half, width), bf16),
        ),
        in_specs=[smem, smem, smem, vmem, vmem, vmem],
        out_specs=(hbm, hbm),
        scratch_shapes=[
            pltpu.VMEM((ranks, 2 * planes, lanes, 128), bf16),
            pltpu.SMEM((4, number), jnp.int32),
            pltpu.SemaphoreType.DMA((4,)),
            pltpu.SemaphoreType.DMA,
        ],
        compiler_params=params,
        name="combine",
    )(named, pair_named, core, mine, theirs, back)
    sums = exchange(sums.reshape(-1, lanes, 128), ("row", "y", "core"))
    sums = sums.reshape(ranks, planes, 2, lanes, 128)

    other = lax.ppermute(passed, "core", swap)
    own = lax.dynamic_index_in_dim(back, index, 1, keepdims=False)
    move = jnp.concatenate(
        [jnp.where(index == 0, own, other), jnp.where(index == 0, other, own)], axis=1
    )
    new = (weight.astype(f32) - step_size * move.astype(f32)).astype(bf16)
    new, sums = lax.optimization_barrier((new, sums))
    mixed = pl.pallas_call(
        project,
        out_shape=jax.ShapeDtypeStruct((width // (2 * planes), tokens.shape[0]), bf16),
        in_specs=[smem, smem, vmem, vmem],
        out_specs=vmem,
        scratch_shapes=[pltpu.VMEM((ranks * rows, 128), bf16)],
        compiler_params=params,
        name="project",
    )(counts, core, tokens, sums)
    return new, mixed.T


def solution(mesh):
    devices = mesh.devices.reshape(mesh.shape["grp"] // 2, 2, mesh.shape["row"])
    inner = Mesh(devices, ("y", "core", "row"))
    group = ("y", "core")
    return jax.shard_map(
        body,
        mesh=inner,
        in_specs=(
            P(group, "row", None),
            P(group, "row", None),
            P(group, None),
            P("row", None),
            P("row"),
        ),
        out_specs=(P(group, "row", None), P("row", group)),
        check_vma=False,
    )
```

time: 125 us -> 120 us (0.960)
  waiting for transfers between devices: 47 us -> 38.8 us
  local copies, waits for them, and re-layouts: 0.73 us -> 4.34 us
  other arithmetic: 3.87 us -> 6 us
    all_to_all x2, waiting for transfers between devices: 44.7 us -> 36.8 us  [exchange(): return lax.all_to_all(data, axes, split_axis=0, concat_axis=0, tiled=True)]
    unnamed x7 -> x10, local copies, waits for them, and re-layouts: 0.73 us -> 2.59 us
    squeeze x0 -> x1, local copies, waits for them, and re-layouts: none -> 1.74 us  [body(): lax.dynamic_index_in_dim(split, 1 - index, 1, keepdims=False)]
    select_n x0 -> x1, other arithmetic: none -> 1.51 us  [body(): jnp.where(index == 0, own, other)]
    ppermute x1 -> x3, starting transfers between devices: 4.3 us -> 3.16 us  [the longest x1 2.45 us: body(): other = lax.ppermute(passed, 'core', swap)]
  transfers between devices with their start and end apart: 3 -> 5, of which waited for: 3 -> 3; matrix products, arithmetic and copies ran while one was open for 0% -> 4% of each run, Pallas kernels for 0% -> 0%
where the time goes in v1:
time: 120 us; the launch traced here: 119 us
  waiting for transfers between devices  38.8 us (32%)
  blocking collectives  35.6 us (30%)
  Pallas kernels  19.4 us (16%)
  starting transfers between devices  14 us (12%)
  other arithmetic  6 us (5%)
  local copies, waits for them, and re-layouts  4.34 us (4%)
  between operations  1.37 us (1%)
    all_to_all x2, waiting for transfers between devices, exchange(): return lax.all_to_all(data, axes, split_axis=0, concat_axis=0, tiled=True)  36.8 us
    all_to_all x1, blocking collectives, exchange(): return lax.all_to_all(data, axes, split_axis=0, concat_axis=0, tiled=True)  35.6 us
    pallas_call x1, Pallas kernels, body(): pl.pallas_call(orthogonalize, out_shape=pltpu.HBM((ranks * rows, width),...  14.4 us
    all_to_all x2, starting transfers between devices, exchange(): return lax.all_to_all(data, axes, split_axis=0, concat_axis=0, tiled=True)  10.8 us
    pallas_call x1, Pallas kernels, body(): pl.pallas_call(combine, out_shape=(pltpu.HBM((ranks, 2 * planes, lanes, 1...  3.57 us
    unnamed x10, local copies, waits for them, and re-layouts  2.59 us
    convert_element_type x1, other arithmetic, body(): whole = exchange(grad.astype(bf16), 'row')  2.47 us
    ppermute x1, starting transfers between devices, body(): other = lax.ppermute(passed, 'core', swap)  2.45 us
  transfers between devices with their start and end apart: 5, of which 3 were waited for; matrix products, arithmetic and copies ran while one was open for 4% of the time, Pallas kernels for 0%

profile of v1, /device:TPU:1, one launch (start us, length us, event | category | flops | bytes accessed | tf_op | source)
XLA Modules:
  0.0 119.5 jit_solution(5022250100482037150)
XLA Ops:
  0.6 2.5 %convert_element_type.13 = bf16[16,128,512]{2,1,0:T(8,128)(2,1)S(1)} convert(f32[16,128,512]{2,1,0:T(8,128)} %param.5) | non-fusion elementwise | flops 1048576 | bytes 6291456 | tf_op jit(solution)/shard_map/convert_element_type | solution.py:135
  3.1 35.6 %all_to_all.15 = bf16[16,128,512]{2,1,0:T(8,128)(2,1)S(1)} all-to-all(bf16[16,128,512]{2,1,0:T(8,128)(2,1)S(1)} %convert_element_type.13), channel_id=1, replica_groups=mesh['y'=4,'core'=2,'row'=16] {'row'}, dimensions={0} | all-to-all | bytes 4194304 | tf_op jit(solution)/shard_map/all_to_all | solution.py:133
  38.7 14.4 %orthogonalize.1 = bf16[2048,512]{1,0:T(8,128)(2,1)} custom-call(bf16[2048,512]{1,0:T(8,128)(2,1)S(1)} %bitcast.22), custom_call_target="tpu_custom_call" | custom-call | tf_op jit(solution)/shard_map/orthogonalize/pallas_call | solution.py:144
  53.1 5.7 %all-to-all-start.1 = ((bf16[32,64,512]{2,1,0:T(8,128)(2,1)}), bf16[32,64,512]{2,1,0:T(8,128)(2,1)S(1)}, u32[]{:S(2)}, u32[]{:S(2)}) async-start(bf16[32,64,512]{2,1,0:T(8,128)(2,1)} %bitcast.27), calls=%async_computation.1 | async-start | bytes 4194304 | tf_op jit(solution)/shard_map/all_to_all | solution.py:133
  58.8 0.0 copy-start.3
  58.8 1.7 %dynamic-slice_bitcast_fusion = (bf16[16,64,512]{2,1,0:T(8,128)(2,1)S(1)}, bf16[16,64,512]{2,1,0:T(8,128)(2,1)S(1)}) fusion(bf16[16,2,64,512]{3,2,1,0:T(8,128)(2,1)} %bitcast.26, s32[]{:T(128)S(6)} %select_n.24, s32[]{:T(128)S(6)} %select_n.23), kind=kLoop, calls=%fused_computation.3 | loop fusion | bytes 4194312 | tf_op jit(solution)/shard_map/jit(dynamic_index_in_dim)/squeeze | solution.py:142
  60.6 0.4 collective-permute-start.1
  61.0 0.3 collective-permute-start
  61.3 2.0 %collective-permute-done.pair_ref = s32[16]{0:T(128)S(1)} collective-permute-done((s32[16]{0:T(128)S(1)}, s32[16]{0:T(128)S(1)}, u32[]{:S(2)}, u32[]{:S(2)}) %collective-permute-start) | collective-permute-done | bytes 96 | tf_op jit(solution)/shard_map/ppermute | solution.py:138
  63.3 0.0 collective-permute-done.1.theirs_ref
  63.3 1.0 copy-done.1
  64.3 22.5 %all-to-all-done.1 = bf16[32,64,512]{2,1,0:T(8,128)(2,1)S(1)} async-done(((bf16[32,64,512]{2,1,0:T(8,128)(2,1)}), bf16[32,64,512]{2,1,0:T(8,128)(2,1)S(1)}, u32[]{:S(2)}, u32[]{:S(2)}) %all-to-all-start.1) | async-done | bytes 2097184 | tf_op jit(solution)/shard_map/all_to_all | solution.py:133
  86.8 1.2 %copy-done.2 = bf16[16,64,512]{2,1,0:T(8,128)(2,1)S(1)} copy-done((bf16[16,64,512]{2,1,0:T(8,128)(2,1)S(1)}, bf16[16,64,512]{2,1,0:T(8,128)(2,1)}, u32[]{:S(2)}) %copy-start.2) | copy-done | bytes 1048600
  88.0 3.6 %combine.1 = (bf16[16,8,32,128]{3,2,1,0:T(8,128)(2,1)}, bf16[16,64,512]{2,1,0:T(8,128)(2,1)}) custom-call(s32[16]{0:T(128)S(1)} %bitcast.25, s32[16]{0:T(128)S(1)} %collective-permute-done.pair_ref, s32[1]{0:T(128)} %bitcast.5.core_ref, bf16[16,64,512]{2,1,0:T(8,128)(2,1)S(1)} %get-tuple-element.13.mine_ref, bf16[16,64,512]{2,1,0:T(8,128)(2,1)S(1)} %copy-done.2, ...), custom_call_target="tpu_custom_call" | custom-call | tf_op jit(solution)/shard_map/combine/pallas_call | solution.py:161
  91.5 2.5 %collective-permute-start.2 = (bf16[16,64,512]{2,1,0:T(8,128)(2,1)}, bf16[16,64,512]{2,1,0:T(8,128)(2,1)}, u32[]{:S(2)}, u32[]{:S(2)}) collective-permute-start(bf16[16,64,512]{2,1,0:T(8,128)(2,1)} %get-tuple-element.6), channel_id=1, source_target_pairs={{0,16},{16,0},{1,17},{17,1},{2,18},{18,2},{3,19},{19,3},{4,20},{20... | collective-permute-start | bytes 3145736 | tf_op jit(solution)/shard_map/ppermute | solution.py:181
  94.0 5.2 %all-to-all-start.2 = ((bf16[128,32,128]{2,1,0:T(8,128)(2,1)}), bf16[128,32,128]{2,1,0:T(8,128)(2,1)S(1)}, u32[]{:S(2)}, u32[]{:S(2)}) async-start(bf16[128,32,128]{2,1,0:T(8,128)(2,1)} %bitcast.28), calls=%async_computation.2 | async-start | bytes 2097152 | tf_op jit(solution)/shard_map/all_to_all | solution.py:133
  99.8 0.0 copy-start.4
  99.8 0.0 collective-permute-done.2
  99.8 1.5 %bitcast_select_fusion.1 = (bf16[16,64,512]{2,1,0:T(8,128)(2,1)S(1)}, bf16[16,64,512]{2,1,0:T(8,128)(2,1)S(1)}) fusion(bf16[16,64,512]{2,1,0:T(8,128)(2,1)} %collective-permute-done.2, pred[]{:T(512)S(6)} %eq.4, bf16[16,2,64,512]{3,2,1,0:T(8,128)(2,1)S(1)} %bitcast.21, s32[]{:T(128)S(6)} %select_n.23), kind=kLoop, calls=%fused_computation.2 | loop fusion | flops 1048576 | bytes 4194309 | tf_op jit(solution)/shard_map/jit(_where)/select_n | solution.py:184
  101.4 0.4 copy-done.4
  101.7 2.0 %subtract_convert_fusion = bf16[16,128,512]{2,1,0:T(8,128)(2,1)} fusion(bf16[16,128,512]{2,1,0:T(8,128)(2,1)S(1)} %copy-done.4, bf16[16,64,512]{2,1,0:T(8,128)(2,1)S(1)} %get-tuple-element.11, bf16[16,64,512]{2,1,0:T(8,128)(2,1)S(1)} %get-tuple-element.10), kind=kLoop, calls=%fused_computation | loop fusion | flops 8388608 | bytes 6291456 | tf_op jit(solution)/shard_map/convert_element_type | solution.py:186
  103.7 14.3 %all-to-all-done.2 = bf16[128,32,128]{2,1,0:T(8,128)(2,1)S(1)} async-done(((bf16[128,32,128]{2,1,0:T(8,128)(2,1)}), bf16[128,32,128]{2,1,0:T(8,128)(2,1)S(1)}, u32[]{:S(2)}, u32[]{:S(2)}) %all-to-all-start.2) | async-done | bytes 1048608 | tf_op jit(solution)/shard_map/all_to_all | solution.py:133
  118.1 0.0 copy-done
  118.1 1.4 %project.1 = bf16[64,384]{1,0:T(8,128)(2,1)} custom-call(s32[1]{0:T(128)S(6)} %copy.11.count_ref, s32[1]{0:T(128)} %bitcast.5.core_ref, bf16[384,2048]{1,0:T(8,128)(2,1)S(1)} %copy-done, bf16[16,4,2,32,128]{4,3,2,1,0:T(8,128)(2,1)S(1)} %bitcast.23), custom_call_target="tpu_custom_call" | custom-call | tf_op jit(solution)/shard_map/project/pallas_call | solution.py:188
  (4 shorter events, 0.0 us)
Async XLA Ops:
  53.1 33.6 %all-to-all-start.1 = ((bf16[32,64,512]{2,1,0:T(8,128)(2,1)}), bf16[32,64,512]{2,1,0:T(8,128)(2,1)S(1)}, u32[]{:S(2)}, u32[]{:S(2)}) async-start(bf16[32,64,512]{2,1,0:T(8,128)(2,1)} %bitcast.27), calls=%async_computation.1 | async-start | bytes 4194304 | tf_op jit(solution)/shard_map/all_to_all | solution.py:133
  58.8 2.2 %copy-start.3 = (s32[16,1]{0,1:T(1,128)S(1)}, s32[16,1]{0,1:T(1,128)}, u32[]{:S(2)}) copy-start(s32[16,1]{0,1:T(1,128)} %param.7) | copy-start | bytes 196
  60.6 2.7 %collective-permute-start.1 = (bf16[16,64,512]{2,1,0:T(8,128)(2,1)S(1)}, bf16[16,64,512]{2,1,0:T(8,128)(2,1)S(1)}, u32[]{:S(2)}, u32[]{:S(2)}) collective-permute-start(bf16[16,64,512]{2,1,0:T(8,128)(2,1)S(1)} %get-tuple-element.12), channel_id=1, source_target_pairs={{0,16},{16,0},{1,17},{17,1},{2,18},{18,2},{3,19},{19,3},{4,20},{20... | collective-permute-start | bytes 3145736 | tf_op jit(solution)/shard_map/ppermute | solution.py:141
  61.0 2.3 %collective-permute-start = (s32[16]{0:T(128)S(1)}, s32[16]{0:T(128)S(1)}, u32[]{:S(2)}, u32[]{:S(2)}) collective-permute-start(s32[16]{0:T(128)S(1)} %bitcast.24), channel_id=1, source_target_pairs={{0,16},{16,0},{1,17},{17,1},{2,18},{18,2},{3,19},{19,3},{4,20},{20... | collective-permute-start | bytes 200 | tf_op jit(solution)/shard_map/ppermute | solution.py:138
  63.3 1.0 copy-start.1
  86.7 1.2 %copy-start.2 = (bf16[16,64,512]{2,1,0:T(8,128)(2,1)S(1)}, bf16[16,64,512]{2,1,0:T(8,128)(2,1)}, u32[]{:S(2)}) copy-start(bf16[16,64,512]{2,1,0:T(8,128)(2,1)} %copy-done.1) | copy-start | bytes 3145732
  91.5 8.3 %collective-permute-start.2 = (bf16[16,64,512]{2,1,0:T(8,128)(2,1)}, bf16[16,64,512]{2,1,0:T(8,128)(2,1)}, u32[]{:S(2)}, u32[]{:S(2)}) collective-permute-start(bf16[16,64,512]{2,1,0:T(8,128)(2,1)} %get-tuple-element.6), channel_id=1, source_target_pairs={{0,16},{16,0},{1,17},{17,1},{2,18},{18,2},{3,19},{19,3},{4,20},{20... | collective-permute-start | bytes 3145736 | tf_op jit(solution)/shard_map/ppermute | solution.py:181
  94.0 24.1 %all-to-all-start.2 = ((bf16[128,32,128]{2,1,0:T(8,128)(2,1)}), bf16[128,32,128]{2,1,0:T(8,128)(2,1)S(1)}, u32[]{:S(2)}, u32[]{:S(2)}) async-start(bf16[128,32,128]{2,1,0:T(8,128)(2,1)} %bitcast.28), calls=%async_computation.2 | async-start | bytes 2097152 | tf_op jit(solution)/shard_map/all_to_all | solution.py:133
  99.8 1.9 %copy-start.4 = (bf16[16,128,512]{2,1,0:T(8,128)(2,1)S(1)}, bf16[16,128,512]{2,1,0:T(8,128)(2,1)}, u32[]{:S(2)}) copy-start(bf16[16,128,512]{2,1,0:T(8,128)(2,1)} %param.6) | copy-start | bytes 6291460
  101.7 16.3 %copy-start = (bf16[384,2048]{1,0:T(8,128)(2,1)S(1)}, bf16[384,2048]{1,0:T(8,128)(2,1)}, u32[]{:S(2)}) copy-start(bf16[384,2048]{1,0:T(8,128)(2,1)} %tokens_ref.1) | copy-start | bytes 4718596

commit v2 on v1

--- a/solution.py
+++ b/solution.py
@@ -56,34 +56,77 @@
         copy.wait()
 
 
+def list_owned(named, table, base):
+    for r in range(named.shape[0]):
+        table[base, r] = -1
+        table[base + 1, r] = -1
+    for e in range(named.shape[0]):
+        o = named[e]
+        seen = table[base, o] >= 0
+        table[base + 1, o] = jnp.where(seen, e, table[base + 1, o])
+        table[base, o] = jnp.where(seen, table[base, o], e)
+
+
+def gather_old(owner_ref, core_ref, weight_ref, keep_ref, send_ref, held, staged, table, *sems):
+    in_sems, out_sems = sems
+    number, rows, width = weight_ref.shape
+    half = rows // 2
+    core = core_ref[0]
+    arriving = []
+    for part in range(4):
+        some = pl.ds(part * (number // 4), number // 4)
+        arriving.append(
+            pltpu.make_async_copy(weight_ref.at[some], held.at[some], in_sems.at[part])
+        )
+        arriving[-1].start()
+    list_owned(owner_ref, table, 0)
+    for copy in arriving:
+        copy.wait()
+    copies = []
+    for place, out_ref in enumerate((send_ref, keep_ref)):
+        near = core if place else 1 - core
+        at = pl.ds(pl.multiple_of(near * half, half), half)
+        for r in range(number):
+            total = 0.0
+            for slot in range(2):
+                e = table[slot, r]
+                old = held[jnp.maximum(e, 0), at, :].astype(f32)
+                total = total + jnp.where(e >= 0, old, 0.0)
+            staged[place, r] = total.astype(bf16)
+        copies.append(pltpu.make_async_copy(staged.at[place], out_ref, out_sems.at[place]))
+        copies[-1].start()
+    for copy in copies:
+        copy.wait()
+
+
 def combine(owner_ref, pair_ref, core_ref, mine_ref, theirs_ref, ortho_ref, *refs):
-    sum_ref, pass_ref, staged, table, sems, pass_sem = refs
+    sum_ref, pass_ref, held, staged, table, in_sems, sems, pass_sem = refs
     number, halves, rows, width = ortho_ref.shape
     lanes = rows // 2
     tiles = width // 128
     core = core_ref[0]
+    arriving = []
+    for part in range(4):
+        some = pl.ds(part * (number // 4), number // 4)
+        arriving.append(pltpu.make_async_copy(mine_ref.at[some], held.at[some], in_sems.at[part]))
+        arriving[-1].start()
     passing = pltpu.make_async_copy(ortho_ref.at[:, 1 - core], pass_ref, pass_sem)
     passing.start()
-    for source, named in enumerate((owner_ref, pair_ref)):
-        for r in range(number):
-            table[2 * source, r] = -1
-            table[2 * source + 1, r] = -1
-        for e in range(number):
-            o = named[e]
-            seen = table[2 * source, o] >= 0
-            table[2 * source + 1, o] = jnp.where(seen, e, table[2 * source + 1, o])
-            table[2 * source, o] = jnp.where(seen, table[2 * source, o], e)
+    list_owned(owner_ref, table, 0)
+    list_owned(pair_ref, table, 2)
 
     low = lax.broadcasted_iota(jnp.int32, (lanes, 128), 1) < 64
     copies = []
     for r in range(number):
-        total = 0.0
+        if r % 4 == 0:
+            arriving[r // 4].wait()
+        move = 0.0
         for slot in range(4):
             e = table[slot, r]
-            at = jnp.maximum(e, 0)
-            old_ref, source = (mine_ref, core) if slot < 2 else (theirs_ref, 1 - core)
-            new = old_ref[at].astype(f32) - step_size * ortho_ref[at, source].astype(f32)
-            total = total + jnp.where(e >= 0, new, 0.0)
+            source = core if slot < 2 else 1 - core
+            one = ortho_ref[jnp.maximum(e, 0), source].astype(f32)
+            move = move + jnp.where(e >= 0, one, 0.0)
+        total = held[r].astype(f32) + theirs_ref[r].astype(f32) - step_size * move
         for t in range(tiles):
             top = total[:lanes, t * 128 : (t + 1) * 128]
             bottom = pltpu.roll(total[lanes:, t * 128 : (t + 1) * 128], 64, 1)
@@ -136,11 +179,26 @@
 
     named = owner[:, 0]
     pair_named = lax.ppermute(named, "core", swap)
-    split = weight.reshape(number, 2, half, width)
-    mine = lax.dynamic_index_in_dim(split, index, 1, keepdims=False)
-    theirs = lax.ppermute(
-        lax.dynamic_index_in_dim(split, 1 - index, 1, keepdims=False), "core", swap
-    )
+    mine, theirs = pl.pallas_call(
+        gather_old,
+        out_shape=(
+            pltpu.HBM((ranks, half, width), bf16),
+            pltpu.HBM((ranks, half, width), bf16),
+        ),
+        in_specs=[smem, smem, hbm],
+        out_specs=(hbm, hbm),
+        scratch_shapes=[
+            pltpu.VMEM((number, rows, width), bf16),
+            pltpu.VMEM((2, ranks, half, width), bf16),
+            pltpu.SMEM((2, number), jnp.int32),
+            pltpu.SemaphoreType.DMA((4,)),
+            pltpu.SemaphoreType.DMA((2,)),
+        ],
+        compiler_params=params,
+        name="gather_old",
+    )(named, core, pltpu.with_memory_space_constraint(weight, pltpu.HBM))
+    theirs = lax.ppermute(theirs, "core", swap)
+
     ortho = pl.pallas_call(
         orthogonalize,
         out_shape=pltpu.HBM((ranks * rows, width), bf16),
@@ -164,17 +222,26 @@
             pltpu.HBM((ranks, 2 * planes, lanes, 128), bf16),
             pltpu.HBM((number, half, width), bf16),
         ),
-        in_specs=[smem, smem, smem, vmem, vmem, vmem],
+        in_specs=[smem, smem, smem, hbm, vmem, vmem],
         out_specs=(hbm, hbm),
         scratch_shapes=[
+            pltpu.VMEM((ranks, half, width), bf16),
             pltpu.VMEM((ranks, 2 * planes, lanes, 128), bf16),
             pltpu.SMEM((4, number), jnp.int32),
             pltpu.SemaphoreType.DMA((4,)),
+            pltpu.SemaphoreType.DMA((4,)),
             pltpu.SemaphoreType.DMA,
         ],
         compiler_params=params,
         name="combine",
-    )(named, pair_named, core, mine, theirs, back)
+    )(
+        named,
+        pair_named,
+        core,
+        pltpu.with_memory_space_constraint(mine, pltpu.HBM),
+        theirs,
+        back,
+    )
     sums = exchange(sums.reshape(-1, lanes, 128), ("row", "y", "core"))
     sums = sums.reshape(ranks, planes, 2, lanes, 128)
 

time: 120 us -> 119 us (level)
  Pallas kernels: 19.4 us -> 23.4 us
  local copies, waits for them, and re-layouts: 4.34 us -> 0.38 us
    pallas_call x0 -> x1, Pallas kernels: none -> 3.87 us  [body(): pl.pallas_call(gather_old, out_shape=(pltpu.HBM((ranks, half, width), bf1...]
    unnamed x10 -> x6, local copies, waits for them, and re-layouts: 2.59 us -> 0.38 us
    squeeze x1 -> x0, local copies, waits for them, and re-layouts: 1.74 us -> none  [body(): lax.dynamic_index_in_dim(split, 1 - index, 1, keepdims=False)]
    all_to_all x2, waiting for transfers between devices: 36.8 us -> 35.4 us  [exchange(): return lax.all_to_all(data, axes, split_axis=0, concat_axis=0, tiled=True)]
  transfers between devices with their start and end apart: 5 -> 5, of which waited for: 3 -> 4; matrix products, arithmetic and copies ran while one was open for 4% -> 3% of each run, Pallas kernels for 0% -> 3%
where the time goes in v2:
time: 119 us; the launch traced here: 118 us
  waiting for transfers between devices  37.7 us (32%)
  blocking collectives  35.6 us (30%)
  Pallas kernels  23.4 us (20%)
  starting transfers between devices  14 us (12%)
  other arithmetic  6 us (5%)
  between operations  1.37 us (1%)
    all_to_all x1, blocking collectives, exchange(): return lax.all_to_all(data, axes, split_axis=0, concat_axis=0, tiled=True)  35.6 us
    all_to_all x2, waiting for transfers between devices, exchange(): return lax.all_to_all(data, axes, split_axis=0, concat_axis=0, tiled=True)  35.4 us
    pallas_call x1, Pallas kernels, body(): pl.pallas_call(orthogonalize, out_shape=pltpu.HBM((ranks * rows, width),...  14.4 us
    all_to_all x2, starting transfers between devices, exchange(): return lax.all_to_all(data, axes, split_axis=0, concat_axis=0, tiled=True)  10.8 us
    pallas_call x1, Pallas kernels, body(): pl.pallas_call(gather_old, out_shape=(pltpu.HBM((ranks, half, width), bf1...  3.87 us
    pallas_call x1, Pallas kernels, body(): pl.pallas_call(combine, out_shape=(pltpu.HBM((ranks, 2 * planes, lanes, 1...  3.7 us
    convert_element_type x1, other arithmetic, body(): whole = exchange(grad.astype(bf16), 'row')  2.47 us
    ppermute x1, starting transfers between devices, body(): other = lax.ppermute(passed, 'core', swap)  2.45 us
  transfers between devices with their start and end apart: 5, of which 4 were waited for; matrix products, arithmetic and copies ran while one was open for 3% of the time, Pallas kernels for 3%

profile of v2, /device:TPU:1, one launch (start us, length us, event | category | flops | bytes accessed | tf_op | source)
XLA Modules:
  0.0 118.4 jit_solution(6936077877623234071)
XLA Ops:
  0.6 2.5 %convert_element_type.13 = bf16[16,128,512]{2,1,0:T(8,128)(2,1)S(1)} convert(f32[16,128,512]{2,1,0:T(8,128)} %param.5) | non-fusion elementwise | flops 1048576 | bytes 6291456 | tf_op jit(solution)/shard_map/convert_element_type | solution.py:178
  3.1 35.6 %all_to_all.15 = bf16[16,128,512]{2,1,0:T(8,128)(2,1)S(1)} all-to-all(bf16[16,128,512]{2,1,0:T(8,128)(2,1)S(1)} %convert_element_type.13), channel_id=1, replica_groups=mesh['y'=4,'core'=2,'row'=16] {'row'}, dimensions={0} | all-to-all | bytes 4194304 | tf_op jit(solution)/shard_map/all_to_all | solution.py:176
  38.7 14.4 %orthogonalize.1 = bf16[2048,512]{1,0:T(8,128)(2,1)} custom-call(bf16[2048,512]{1,0:T(8,128)(2,1)S(1)} %bitcast.13), custom_call_target="tpu_custom_call" | custom-call | tf_op jit(solution)/shard_map/orthogonalize/pallas_call | solution.py:202
  53.1 0.0 copy-start.1
  53.1 5.7 %all-to-all-start.1 = ((bf16[32,64,512]{2,1,0:T(8,128)(2,1)}), bf16[32,64,512]{2,1,0:T(8,128)(2,1)S(1)}, u32[]{:S(2)}, u32[]{:S(2)}) async-start(bf16[32,64,512]{2,1,0:T(8,128)(2,1)} %bitcast.18), calls=%async_computation.1 | async-start | bytes 4194304 | tf_op jit(solution)/shard_map/all_to_all | solution.py:176
  58.8 0.0 copy-done.1
  58.8 3.9 %gather_old.1 = (bf16[16,64,512]{2,1,0:T(8,128)(2,1)}, bf16[16,64,512]{2,1,0:T(8,128)(2,1)}) custom-call(s32[16]{0:T(128)S(1)} %bitcast.15, s32[1]{0:T(128)} %bitcast.5.core_ref, bf16[16,128,512]{2,1,0:T(8,128)(2,1)} %weight_ref.1), custom_call_target="tpu_custom_call" | custom-call | tf_op jit(solution)/shard_map/gather_old/pallas_call | solution.py:182
  62.7 0.4 collective-permute-start.1
  63.1 0.3 collective-permute-start
  63.4 2.0 %collective-permute-done.pair_ref = s32[16]{0:T(128)S(1)} collective-permute-done((s32[16]{0:T(128)S(1)}, s32[16]{0:T(128)S(1)}, u32[]{:S(2)}, u32[]{:S(2)}) %collective-permute-start) | collective-permute-done | bytes 96 | tf_op jit(solution)/shard_map/ppermute | solution.py:181
  65.4 0.2 collective-permute-done.1.theirs_ref
  65.7 21.1 %all-to-all-done.1 = bf16[32,64,512]{2,1,0:T(8,128)(2,1)S(1)} async-done(((bf16[32,64,512]{2,1,0:T(8,128)(2,1)}), bf16[32,64,512]{2,1,0:T(8,128)(2,1)S(1)}, u32[]{:S(2)}, u32[]{:S(2)}) %all-to-all-start.1) | async-done | bytes 2097184 | tf_op jit(solution)/shard_map/all_to_all | solution.py:176
  86.8 3.7 %combine.1 = (bf16[16,8,32,128]{3,2,1,0:T(8,128)(2,1)}, bf16[16,64,512]{2,1,0:T(8,128)(2,1)}) custom-call(s32[16]{0:T(128)S(1)} %bitcast.17, s32[16]{0:T(128)S(1)} %collective-permute-done.pair_ref, s32[1]{0:T(128)} %bitcast.5.core_ref, bf16[16,64,512]{2,1,0:T(8,128)(2,1)} %get-tuple-element.8.mine_ref, ...), custom_call_target="tpu_custom_call" | custom-call | tf_op jit(solution)/shard_map/combine/pallas_call | solution.py:219
  90.5 2.5 %collective-permute-start.2 = (bf16[16,64,512]{2,1,0:T(8,128)(2,1)}, bf16[16,64,512]{2,1,0:T(8,128)(2,1)}, u32[]{:S(2)}, u32[]{:S(2)}) collective-permute-start(bf16[16,64,512]{2,1,0:T(8,128)(2,1)} %get-tuple-element.10), channel_id=1, source_target_pairs={{0,16},{16,0},{1,17},{17,1},{2,18},{18,2},{3,19},{19,3},{4,20},{20... | collective-permute-start | bytes 3145736 | tf_op jit(solution)/shard_map/ppermute | solution.py:248
  92.9 5.2 %all-to-all-start.2 = ((bf16[128,32,128]{2,1,0:T(8,128)(2,1)}), bf16[128,32,128]{2,1,0:T(8,128)(2,1)S(1)}, u32[]{:S(2)}, u32[]{:S(2)}) async-start(bf16[128,32,128]{2,1,0:T(8,128)(2,1)} %bitcast.19), calls=%async_computation.2 | async-start | bytes 2097152 | tf_op jit(solution)/shard_map/all_to_all | solution.py:176
  98.8 0.0 copy-start.2
  98.8 0.0 collective-permute-done.2
  98.8 1.5 %bitcast_select_fusion.1 = (bf16[16,64,512]{2,1,0:T(8,128)(2,1)S(1)}, bf16[16,64,512]{2,1,0:T(8,128)(2,1)S(1)}) fusion(bf16[16,64,512]{2,1,0:T(8,128)(2,1)} %collective-permute-done.2, pred[]{:T(512)S(6)} %eq.4, bf16[16,2,64,512]{3,2,1,0:T(8,128)(2,1)S(1)} %bitcast.12, s32[]{:T(128)S(6)} %select_n.19), kind=kLoop, calls=%fused_computation.2 | loop fusion | flops 1048576 | bytes 4194309 | tf_op jit(solution)/shard_map/jit(_where)/select_n | solution.py:251
  100.3 0.4 copy-done.2
  100.7 0.0 copy-start
  100.7 2.0 %subtract_convert_fusion = bf16[16,128,512]{2,1,0:T(8,128)(2,1)} fusion(bf16[16,128,512]{2,1,0:T(8,128)(2,1)S(1)} %copy-done.2, bf16[16,64,512]{2,1,0:T(8,128)(2,1)S(1)} %get-tuple-element.15, bf16[16,64,512]{2,1,0:T(8,128)(2,1)S(1)} %get-tuple-element.14), kind=kLoop, calls=%fused_computation | loop fusion | flops 8388608 | bytes 6291456 | tf_op jit(solution)/shard_map/convert_element_type | solution.py:253
  102.7 14.3 %all-to-all-done.2 = bf16[128,32,128]{2,1,0:T(8,128)(2,1)S(1)} async-done(((bf16[128,32,128]{2,1,0:T(8,128)(2,1)}), bf16[128,32,128]{2,1,0:T(8,128)(2,1)S(1)}, u32[]{:S(2)}, u32[]{:S(2)}) %all-to-all-start.2) | async-done | bytes 1048608 | tf_op jit(solution)/shard_map/all_to_all | solution.py:176
  117.0 0.0 copy-done
  117.0 1.4 %project.1 = bf16[64,384]{1,0:T(8,128)(2,1)} custom-call(s32[1]{0:T(128)S(6)} %copy.7.count_ref, s32[1]{0:T(128)} %bitcast.5.core_ref, bf16[384,2048]{1,0:T(8,128)(2,1)S(1)} %copy-done, bf16[16,4,2,32,128]{4,3,2,1,0:T(8,128)(2,1)S(1)} %bitcast.14), custom_call_target="tpu_custom_call" | custom-call | tf_op jit(solution)/shard_map/project/pallas_call | solution.py:255
Async XLA Ops:
  53.1 5.7 %copy-start.1 = (s32[16,1]{0,1:T(1,128)S(1)}, s32[16,1]{0,1:T(1,128)}, u32[]{:S(2)}) copy-start(s32[16,1]{0,1:T(1,128)} %param.7) | copy-start | bytes 196
  53.1 33.6 %all-to-all-start.1 = ((bf16[32,64,512]{2,1,0:T(8,128)(2,1)}), bf16[32,64,512]{2,1,0:T(8,128)(2,1)S(1)}, u32[]{:S(2)}, u32[]{:S(2)}) async-start(bf16[32,64,512]{2,1,0:T(8,128)(2,1)} %bitcast.18), calls=%async_computation.1 | async-start | bytes 4194304 | tf_op jit(solution)/shard_map/all_to_all | solution.py:176
  62.7 3.0 %collective-permute-start.1 = (bf16[16,64,512]{2,1,0:T(8,128)(2,1)}, bf16[16,64,512]{2,1,0:T(8,128)(2,1)S(1)}, u32[]{:S(2)}, u32[]{:S(2)}) collective-permute-start(bf16[16,64,512]{2,1,0:T(8,128)(2,1)} %get-tuple-element.9), channel_id=1, source_target_pairs={{0,16},{16,0},{1,17},{17,1},{2,18},{18,2},{3,19},{19,3},{4,20},{20... | collective-permute-start | bytes 3145736 | tf_op jit(solution)/shard_map/ppermute | solution.py:200
  63.1 2.3 %collective-permute-start = (s32[16]{0:T(128)S(1)}, s32[16]{0:T(128)S(1)}, u32[]{:S(2)}, u32[]{:S(2)}) collective-permute-start(s32[16]{0:T(128)S(1)} %bitcast.16), channel_id=1, source_target_pairs={{0,16},{16,0},{1,17},{17,1},{2,18},{18,2},{3,19},{19,3},{4,20},{20... | collective-permute-start | bytes 200 | tf_op jit(solution)/shard_map/ppermute | solution.py:181
  90.5 8.3 %collective-permute-start.2 = (bf16[16,64,512]{2,1,0:T(8,128)(2,1)}, bf16[16,64,512]{2,1,0:T(8,128)(2,1)}, u32[]{:S(2)}, u32[]{:S(2)}) collective-permute-start(bf16[16,64,512]{2,1,0:T(8,128)(2,1)} %get-tuple-element.10), channel_id=1, source_target_pairs={{0,16},{16,0},{1,17},{17,1},{2,18},{18,2},{3,19},{19,3},{4,20},{20... | collective-permute-start | bytes 3145736 | tf_op jit(solution)/shard_map/ppermute | solution.py:248
  92.9 24.1 %all-to-all-start.2 = ((bf16[128,32,128]{2,1,0:T(8,128)(2,1)}), bf16[128,32,128]{2,1,0:T(8,128)(2,1)S(1)}, u32[]{:S(2)}, u32[]{:S(2)}) async-start(bf16[128,32,128]{2,1,0:T(8,128)(2,1)} %bitcast.19), calls=%async_computation.2 | async-start | bytes 2097152 | tf_op jit(solution)/shard_map/all_to_all | solution.py:176
  98.8 1.9 %copy-start.2 = (bf16[16,128,512]{2,1,0:T(8,128)(2,1)S(1)}, bf16[16,128,512]{2,1,0:T(8,128)(2,1)}, u32[]{:S(2)}) copy-start(bf16[16,128,512]{2,1,0:T(8,128)(2,1)} %weight_ref.1) | copy-start | bytes 6291460
  100.7 16.3 %copy-start = (bf16[384,2048]{1,0:T(8,128)(2,1)S(1)}, bf16[384,2048]{1,0:T(8,128)(2,1)}, u32[]{:S(2)}) copy-start(bf16[384,2048]{1,0:T(8,128)(2,1)} %tokens_ref.1) | copy-start | bytes 4718596

commit v3 on v2

--- a/solution.py
+++ b/solution.py
@@ -11,9 +11,24 @@
 coef_b = -4.775
 coef_c = 2.0315
 step_size = 0.5
+PIECES = 2
 
 f32 = jnp.float32
 bf16 = jnp.bfloat16
+
+
+def narrow(far_ref, out_ref, held, sems):
+    parts = sems.shape[0]
+    size = out_ref.shape[0] // parts
+    copies = []
+    for part in range(parts):
+        some = pl.ds(part * size, size)
+        copies.append(pltpu.make_async_copy(far_ref.at[some], held.at[some], sems.at[part]))
+        copies[-1].start()
+    for part in range(parts):
+        copies[part].wait()
+        some = pl.ds(part * size, size)
+        out_ref[some] = held[some].astype(bf16)
 
 
 def orthogonalize(x_ref, out_ref, held, staged, sems):
@@ -56,18 +71,18 @@
         copy.wait()
 
 
-def list_owned(named, table, base):
+def list_owned(named, table):
     for r in range(named.shape[0]):
-        table[base, r] = -1
-        table[base + 1, r] = -1
+        table[0, r] = -1
+        table[1, r] = -1
     for e in range(named.shape[0]):
         o = named[e]
-        seen = table[base, o] >= 0
-        table[base + 1, o] = jnp.where(seen, e, table[base + 1, o])
-        table[base, o] = jnp.where(seen, table[base, o], e)
-
-
-def gather_old(owner_ref, core_ref, weight_ref, keep_ref, send_ref, held, staged, table, *sems):
+        seen = table[0, o] >= 0
+        table[1, o] = jnp.where(seen, e, table[1, o])
+        table[0, o] = jnp.where(seen, table[0, o], e)
+
+
+def gather_old(owner_ref, core_ref, weight_ref, keep_ref, send_ref, table, held, staged, *sems):
     in_sems, out_sems = sems
     number, rows, width = weight_ref.shape
     half = rows // 2
@@ -79,7 +94,7 @@
             pltpu.make_async_copy(weight_ref.at[some], held.at[some], in_sems.at[part])
         )
         arriving[-1].start()
-    list_owned(owner_ref, table, 0)
+    list_owned(owner_ref, table)
     for copy in arriving:
         copy.wait()
     copies = []
@@ -99,48 +114,48 @@
         copy.wait()
 
 
-def combine(owner_ref, pair_ref, core_ref, mine_ref, theirs_ref, ortho_ref, *refs):
-    sum_ref, pass_ref, held, staged, table, in_sems, sems, pass_sem = refs
+def combine(table_ref, pair_ref, core_ref, old_ref, ortho_ref, *refs):
+    sum_ref, pass_refs, (staged, sems, pass_sems) = refs[0], refs[1:-3], refs[-3:]
     number, halves, rows, width = ortho_ref.shape
     lanes = rows // 2
     tiles = width // 128
     core = core_ref[0]
-    arriving = []
-    for part in range(4):
-        some = pl.ds(part * (number // 4), number // 4)
-        arriving.append(pltpu.make_async_copy(mine_ref.at[some], held.at[some], in_sems.at[part]))
-        arriving[-1].start()
-    passing = pltpu.make_async_copy(ortho_ref.at[:, 1 - core], pass_ref, pass_sem)
-    passing.start()
-    list_owned(owner_ref, table, 0)
-    list_owned(pair_ref, table, 2)
-
+    passing = []
+    for part, pass_ref in enumerate(pass_refs):
+        some = pl.ds(part * pass_ref.shape[0], pass_ref.shape[0])
+        passing.append(
+            pltpu.make_async_copy(ortho_ref.at[some, 1 - core], pass_ref, pass_sems.at[part])
+        )
+        passing[-1].start()
     low = lax.broadcasted_iota(jnp.int32, (lanes, 128), 1) < 64
     copies = []
     for r in range(number):
-        if r % 4 == 0:
-            arriving[r // 4].wait()
-        move = 0.0
+        slots = []
         for slot in range(4):
-            e = table[slot, r]
+            e = (table_ref if slot < 2 else pair_ref)[slot % 2, r]
             source = core if slot < 2 else 1 - core
-            one = ortho_ref[jnp.maximum(e, 0), source].astype(f32)
-            move = move + jnp.where(e >= 0, one, 0.0)
-        total = held[r].astype(f32) + theirs_ref[r].astype(f32) - step_size * move
+            slots.append((e >= 0, jnp.maximum(e, 0), source))
         for t in range(tiles):
-            top = total[:lanes, t * 128 : (t + 1) * 128]
-            bottom = pltpu.roll(total[lanes:, t * 128 : (t + 1) * 128], 64, 1)
+            columns = slice(t * 128, (t + 1) * 128)
+            move = 0.0
+            for listed, at, source in slots:
+                one = ortho_ref[at, source, :, columns].astype(f32)
+                move = move + jnp.where(listed, one, 0.0)
+            total = old_ref[r, :, columns].astype(f32) - step_size * move
+            top = total[:lanes]
+            bottom = pltpu.roll(total[lanes:], 64, 1)
             staged[r, 2 * t] = jnp.where(low, top, bottom).astype(bf16)
             staged[r, 2 * t + 1] = jnp.where(low, bottom, top).astype(bf16)
-        if r % 4 == 3:
-            ready = pl.ds(r - 3, 4)
+        if r % 2 == 1:
+            ready = pl.ds(r - 1, 2)
             copies.append(
-                pltpu.make_async_copy(staged.at[ready], sum_ref.at[ready], sems.at[r // 4])
+                pltpu.make_async_copy(staged.at[ready], sum_ref.at[ready], sems.at[r // 2])
             )
             copies[-1].start()
     for copy in copies:
         copy.wait()
-    passing.wait()
+    for copy in passing:
+        copy.wait()
 
 
 def project(count_ref, core_ref, tokens_ref, sums_ref, out_ref, held):
@@ -175,22 +190,30 @@
     def exchange(data, axes):
         return lax.all_to_all(data, axes, split_axis=0, concat_axis=0, tiled=True)
 
-    whole = exchange(grad.astype(bf16), "row")
+    narrowed = pl.pallas_call(
+        narrow,
+        out_shape=jax.ShapeDtypeStruct(grad.shape, bf16),
+        in_specs=[hbm],
+        out_specs=vmem,
+        scratch_shapes=[pltpu.VMEM(grad.shape, f32), pltpu.SemaphoreType.DMA((16,))],
+        compiler_params=params,
+        name="narrow",
+    )(pltpu.with_memory_space_constraint(grad, pltpu.HBM))
+    whole = exchange(narrowed, "row")
 
     named = owner[:, 0]
-    pair_named = lax.ppermute(named, "core", swap)
-    mine, theirs = pl.pallas_call(
+    mine, theirs, table = pl.pallas_call(
         gather_old,
         out_shape=(
             pltpu.HBM((ranks, half, width), bf16),
             pltpu.HBM((ranks, half, width), bf16),
+            jax.ShapeDtypeStruct((2, number), jnp.int32),
         ),
         in_specs=[smem, smem, hbm],
-        out_specs=(hbm, hbm),
+        out_specs=(hbm, hbm, smem),
         scratch_shapes=[
             pltpu.VMEM((number, rows, width), bf16),
             pltpu.VMEM((2, ranks, half, width), bf16),
-            pltpu.SMEM((2, number), jnp.int32),
             pltpu.SemaphoreType.DMA((4,)),
             pltpu.SemaphoreType.DMA((2,)),
         ],
@@ -198,6 +221,8 @@
         name="gather_old",
     )(named, core, pltpu.with_memory_space_constraint(weight, pltpu.HBM))
     theirs = lax.ppermute(theirs, "core", swap)
+    pair_table = lax.ppermute(table, "core", swap)
+    old = (mine.astype(f32) + theirs.astype(f32)).astype(bf16)
 
     ortho = pl.pallas_call(
         orthogonalize,
@@ -216,41 +241,37 @@
     back = back.reshape(number, 2, half, width)
 
     lanes = half // 2
-    sums, passed = pl.pallas_call(
+    sums, *passed = pl.pallas_call(
         combine,
         out_shape=(
             pltpu.HBM((ranks, 2 * planes, lanes, 128), bf16),
-            pltpu.HBM((number, half, width), bf16),
+            *[pltpu.HBM((number // PIECES, half, width), bf16) for _ in range(PIECES)],
         ),
-        in_specs=[smem, smem, smem, hbm, vmem, vmem],
-        out_specs=(hbm, hbm),
+        in_specs=[smem, smem, smem, vmem, vmem],
+        out_specs=(hbm,) * (1 + PIECES),
         scratch_shapes=[
-            pltpu.VMEM((ranks, half, width), bf16),
             pltpu.VMEM((ranks, 2 * planes, lanes, 128), bf16),
-            pltpu.SMEM((4, number), jnp.int32),
-            pltpu.SemaphoreType.DMA((4,)),
-            pltpu.SemaphoreType.DMA((4,)),
-            pltpu.SemaphoreType.DMA,
+            pltpu.SemaphoreType.DMA((8,)),
+            pltpu.SemaphoreType.DMA((PIECES,)),
         ],
         compiler_params=params,
         name="combine",
     )(
-        named,
-        pair_named,
+        table,
+        pair_table,
         core,
-        pltpu.with_memory_space_constraint(mine, pltpu.HBM),
-        theirs,
+        old,
         back,
     )
     sums = exchange(sums.reshape(-1, lanes, 128), ("row", "y", "core"))
     sums = sums.reshape(ranks, planes, 2, lanes, 128)
 
-    other = lax.ppermute(passed, "core", swap)
-    own = lax.dynamic_index_in_dim(back, index, 1, keepdims=False)
-    move = jnp.concatenate(
-        [jnp.where(index == 0, own, other), jnp.where(index == 0, other, own)], axis=1
-    )
-    new = (weight.astype(f32) - step_size * move.astype(f32)).astype(bf16)
+    other = jnp.concatenate([lax.ppermute(piece, "core", swap) for piece in passed])
+    own = lax.dynamic_index_in_dim(back, index, 1, keepdims=True)
+    near = lax.broadcasted_iota(jnp.int32, (1, 2, 1, 1), 1) == index
+    move = jnp.where(near, own, other[:, None])
+    new = weight.reshape(move.shape).astype(f32) - step_size * move.astype(f32)
+    new = new.astype(bf16).reshape(weight.shape)
     new, sums = lax.optimization_barrier((new, sums))
     mixed = pl.pallas_call(
         project,

time: 119 us -> 117 us (0.983)
  waiting for transfers between devices: 37.7 us -> 33.7 us
  Pallas kernels: 23.4 us -> 25.3 us
    all_to_all x2, waiting for transfers between devices: 35.4 us -> 29.8 us  [exchange(): return lax.all_to_all(data, axes, split_axis=0, concat_axis=0, tiled=True)]
    pallas_call x0 -> x1, Pallas kernels: none -> 2.29 us  [body(): pl.pallas_call(narrow, out_shape=jax.ShapeDtypeStruct(grad.shape, bf16),...]
    ppermute x1, waiting for transfers between devices: 0.23 us -> 2.36 us  [body(): theirs = lax.ppermute(theirs, 'core', swap)]
    all_to_all x2, starting transfers between devices: 10.8 us -> 12.8 us  [exchange(): return lax.all_to_all(data, axes, split_axis=0, concat_axis=0, tiled=True)]
    select_n x1 -> x0, other arithmetic: 1.51 us -> none  [body(): jnp.where(index == 0, own, other)]
    ppermute x2 -> x3, starting transfers between devices: 2.73 us -> 1.4 us  [the longest x2 1.24 us: body(): lax.ppermute(piece, 'core', swap)]
    concatenate x0 -> x1, other arithmetic: none -> 1.29 us  [body(): jnp.concatenate([lax.ppermute(piece, 'core', swap) for piece in passed])]
  transfers between devices with their start and end apart: 5 -> 6, of which waited for: 4 -> 5; matrix products, arithmetic and copies ran while one was open for 3% -> 5% of each run, Pallas kernels for 3% -> 4%
where the time goes in v3:
time: 117 us
  blocking collectives  35.6 us (30%)
  waiting for transfers between devices  33.7 us (29%)
  Pallas kernels  25.3 us (22%)
  starting transfers between devices  14.8 us (13%)
  other arithmetic  5.68 us (5%)
  between operations  1.41 us (1%)
    all_to_all x1, blocking collectives, exchange(): return lax.all_to_all(data, axes, split_axis=0, concat_axis=0, tiled=True)  35.6 us
    all_to_all x2, waiting for transfers between devices, exchange(): return lax.all_to_all(data, axes, split_axis=0, concat_axis=0, tiled=True)  29.8 us
    pallas_call x1, Pallas kernels, body(): pl.pallas_call(orthogonalize, out_shape=pltpu.HBM((ranks * rows, width),...  14.4 us
    all_to_all x2, starting transfers between devices, exchange(): return lax.all_to_all(data, axes, split_axis=0, concat_axis=0, tiled=True)  12.8 us
    pallas_call x1, Pallas kernels, body(): pl.pallas_call(gather_old, out_shape=(pltpu.HBM((ranks, half, width), bf1...  4.44 us
    convert_element_type x1, other arithmetic, body(): new = new.astype(bf16).reshape(weight.shape)  2.83 us
    pallas_call x1, Pallas kernels, body(): pl.pallas_call(combine, out_shape=(pltpu.HBM((ranks, 2 * planes, lanes, 1...  2.79 us
    ppermute x1, waiting for transfers between devices, body(): theirs = lax.ppermute(theirs, 'core', swap)  2.36 us
  transfers between devices with their start and end apart: 6, of which 5 were waited for; matrix products, arithmetic and copies ran while one was open for 5% of the time, Pallas kernels for 4%

profile of v3, /device:TPU:1, one launch (start us, length us, event | category | flops | bytes accessed | tf_op | source)
XLA Modules:
  0.0 116.8 jit_solution(13814828249446671026)
XLA Ops:
  0.6 2.3 %narrow.1 = bf16[16,128,512]{2,1,0:T(8,128)(2,1)S(1)} custom-call(f32[16,128,512]{2,1,0:T(8,128)} %far_ref.1), custom_call_target="tpu_custom_call" | custom-call | tf_op jit(solution)/shard_map/narrow/pallas_call | solution.py:193
  2.9 35.6 %all_to_all.15 = bf16[16,128,512]{2,1,0:T(8,128)(2,1)S(1)} all-to-all(bf16[16,128,512]{2,1,0:T(8,128)(2,1)S(1)} %narrow.1), channel_id=1, replica_groups=mesh['y'=4,'core'=2,'row'=16] {'row'}, dimensions={0} | all-to-all | bytes 4194304 | tf_op jit(solution)/shard_map/all_to_all | solution.py:191
  38.5 14.4 %orthogonalize.1 = bf16[2048,512]{1,0:T(8,128)(2,1)} custom-call(bf16[2048,512]{1,0:T(8,128)(2,1)S(1)} %bitcast.18), custom_call_target="tpu_custom_call" | custom-call | tf_op jit(solution)/shard_map/orthogonalize/pallas_call | solution.py:227
  52.9 0.0 copy-start.1
  53.0 5.7 %all-to-all-start.1 = ((bf16[32,64,512]{2,1,0:T(8,128)(2,1)}), bf16[32,64,512]{2,1,0:T(8,128)(2,1)S(1)}, u32[]{:S(2)}, u32[]{:S(2)}) async-start(bf16[32,64,512]{2,1,0:T(8,128)(2,1)} %bitcast.21), calls=%async_computation.1 | async-start | bytes 4194304 | tf_op jit(solution)/shard_map/all_to_all | solution.py:191
  58.6 4.4 %gather_old.1 = (bf16[16,64,512]{2,1,0:T(8,128)(2,1)}, bf16[16,64,512]{2,1,0:T(8,128)(2,1)}, s32[2,16]{1,0:T(2,128)S(1)}) custom-call(s32[16]{0:T(128)S(1)} %bitcast.20, s32[1]{0:T(128)} %bitcast.6.core_ref, bf16[16,128,512]{2,1,0:T(8,128)(2,1)} %weight_ref.1), custom_call_target="tpu_custom_call" | custom-call | tf_op jit(solution)/shard_map/gather_old/pallas_call | solution.py:205
  63.1 0.6 collective-permute-start.1
  63.7 0.2 collective-permute-start
  63.9 2.4 %collective-permute-done.1 = bf16[16,64,512]{2,1,0:T(8,128)(2,1)S(1)} collective-permute-done((bf16[16,64,512]{2,1,0:T(8,128)(2,1)}, bf16[16,64,512]{2,1,0:T(8,128)(2,1)S(1)}, u32[]{:S(2)}, u32[]{:S(2)}) %collective-permute-start.1) | collective-permute-done | bytes 1048608 | tf_op jit(solution)/shard_map/ppermute | solution.py:223
  66.2 1.5 %add_convert_fusion.old_ref = bf16[16,64,512]{2,1,0:T(8,128)(2,1)S(1)} fusion(bf16[16,64,512]{2,1,0:T(8,128)(2,1)S(1)} %collective-permute-done.1, bf16[16,64,512]{2,1,0:T(8,128)(2,1)} %get-tuple-element.11), kind=kLoop, calls=%fused_computation.2 | loop fusion | flops 2097152 | bytes 3145728 | tf_op jit(solution)/shard_map/convert_element_type | solution.py:225
  67.8 18.8 %all-to-all-done.1 = bf16[32,64,512]{2,1,0:T(8,128)(2,1)S(1)} async-done(((bf16[32,64,512]{2,1,0:T(8,128)(2,1)}), bf16[32,64,512]{2,1,0:T(8,128)(2,1)S(1)}, u32[]{:S(2)}, u32[]{:S(2)}) %all-to-all-start.1) | async-done | bytes 2097184 | tf_op jit(solution)/shard_map/all_to_all | solution.py:191
  86.6 2.8 %combine.1 = (bf16[16,8,32,128]{3,2,1,0:T(8,128)(2,1)}, bf16[8,64,512]{2,1,0:T(8,128)(2,1)}, bf16[8,64,512]{2,1,0:T(8,128)(2,1)}) custom-call(s32[2,16]{1,0:T(2,128)S(1)} %get-tuple-element.10.table_ref, s32[2,16]{1,0:T(2,128)S(1)} %collective-permute-done.pair_ref, s32[1]{0:T(128)} %bitcast.6.core_ref, bf16[16,64,512]{2,1,0:T(8,128)(2,1)S(1)} %add_convert_fusion.old_ref, ...), custom_call_target="tpu_custom_call" | custom-call | tf_op jit(solution)/shard_map/combine/pallas_call | solution.py:244
  89.4 7.1 %all-to-all-start.2 = ((bf16[128,32,128]{2,1,0:T(8,128)(2,1)}), bf16[128,32,128]{2,1,0:T(8,128)(2,1)S(1)}, u32[]{:S(2)}, u32[]{:S(2)}) async-start(bf16[128,32,128]{2,1,0:T(8,128)(2,1)} %bitcast.22), calls=%async_computation.2 | async-start | bytes 2097152 | tf_op jit(solution)/shard_map/all_to_all | solution.py:191
  96.5 1.1 collective-permute-start.2
  97.7 0.1 collective-permute-start.3
  97.8 0.1 broadcast_in_dim.38
  97.9 0.1 broadcast_in_dim.39
  98.6 0.1 dynamic-slice_bitcast_fusion
  98.7 0.9 collective-permute-done.2
  99.6 0.7 collective-permute-done.3
  100.3 1.3 %pad_maximum_fusion = bf16[16,64,512]{2,1,0:T(8,128)(2,1)S(1)} fusion(bf16[8,64,512]{2,1,0:T(8,128)(2,1)} %collective-permute-done.3, bf16[8,64,512]{2,1,0:T(8,128)(2,1)} %collective-permute-done.2), kind=kLoop, calls=%fused_computation.3 | loop fusion | flops 524288 | bytes 2097152 | tf_op jit(solution)/shard_map/concatenate | solution.py:269
  101.6 2.8 %subtract_convert_fusion = bf16[16,128,512]{2,1,0:T(8,128)(2,1)} fusion(bf16[16,128,512]{2,1,0:T(8,128)(2,1)S(1)} %copy-done.2, pred[128]{0:T(512)(128)(4,1)S(1)} %broadcast_in_dim.39, bf16[16,64,512]{2,1,0:T(8,128)(2,1)S(1)} %pad_maximum_fusion, bf16[16,64,512]{2,1,0:T(8,128)(2,1)S(1)} %dynamic-slice_bitcast_fusion), kind=kLoop, calls=%fused_computation | loop fusion | flops 6291456 | bytes 6291584 | tf_op jit(solution)/shard_map/convert_element_type | solution.py:274
  104.5 11.0 %all-to-all-done.2 = bf16[128,32,128]{2,1,0:T(8,128)(2,1)S(1)} async-done(((bf16[128,32,128]{2,1,0:T(8,128)(2,1)}), bf16[128,32,128]{2,1,0:T(8,128)(2,1)S(1)}, u32[]{:S(2)}, u32[]{:S(2)}) %all-to-all-start.2) | async-done | bytes 1048608 | tf_op jit(solution)/shard_map/all_to_all | solution.py:191
  115.4 1.4 %project.1 = bf16[64,384]{1,0:T(8,128)(2,1)} custom-call(s32[1]{0:T(128)S(6)} %copy.7.count_ref, s32[1]{0:T(128)} %bitcast.6.core_ref, bf16[384,2048]{1,0:T(8,128)(2,1)S(1)} %copy-done, bf16[16,4,2,32,128]{4,3,2,1,0:T(8,128)(2,1)S(1)} %bitcast.19), custom_call_target="tpu_custom_call" | custom-call | tf_op jit(solution)/shard_map/project/pallas_call | solution.py:276
  (7 shorter events, 0.0 us)
Async XLA Ops:
  52.9 5.7 %copy-start.1 = (s32[16,1]{0,1:T(1,128)S(1)}, s32[16,1]{0,1:T(1,128)}, u32[]{:S(2)}) copy-start(s32[16,1]{0,1:T(1,128)} %param.7) | copy-start | bytes 196
  53.0 33.6 %all-to-all-start.1 = ((bf16[32,64,512]{2,1,0:T(8,128)(2,1)}), bf16[32,64,512]{2,1,0:T(8,128)(2,1)S(1)}, u32[]{:S(2)}, u32[]{:S(2)}) async-start(bf16[32,64,512]{2,1,0:T(8,128)(2,1)} %bitcast.21), calls=%async_computation.1 | async-start | bytes 4194304 | tf_op jit(solution)/shard_map/all_to_all | solution.py:191
  63.1 3.1 %collective-permute-start.1 = (bf16[16,64,512]{2,1,0:T(8,128)(2,1)}, bf16[16,64,512]{2,1,0:T(8,128)(2,1)S(1)}, u32[]{:S(2)}, u32[]{:S(2)}) collective-permute-start(bf16[16,64,512]{2,1,0:T(8,128)(2,1)} %get-tuple-element.12), channel_id=1, source_target_pairs={{0,16},{16,0},{1,17},{17,1},{2,18},{18,2},{3,19},{19,3},{4,20},{20... | collective-permute-start | bytes 3145736 | tf_op jit(solution)/shard_map/ppermute | solution.py:223
  63.7 4.1 %collective-permute-start = (s32[2,16]{1,0:T(2,128)S(1)}, s32[2,16]{1,0:T(2,128)S(1)}, u32[]{:S(2)}, u32[]{:S(2)}) collective-permute-start(s32[2,16]{1,0:T(2,128)S(1)} %get-tuple-element.10.table_ref), channel_id=1, source_target_pairs={{0,16},{16,0},{1,17},{17,1},{2,18},{18,2},{3,19},{19,3},{4,20},{20... | collective-permute-start | bytes 392 | tf_op jit(solution)/shard_map/ppermute | solution.py:224
  89.4 26.1 %all-to-all-start.2 = ((bf16[128,32,128]{2,1,0:T(8,128)(2,1)}), bf16[128,32,128]{2,1,0:T(8,128)(2,1)S(1)}, u32[]{:S(2)}, u32[]{:S(2)}) async-start(bf16[128,32,128]{2,1,0:T(8,128)(2,1)} %bitcast.22), calls=%async_computation.2 | async-start | bytes 2097152 | tf_op jit(solution)/shard_map/all_to_all | solution.py:191
  96.5 3.0 %collective-permute-start.2 = (bf16[8,64,512]{2,1,0:T(8,128)(2,1)}, bf16[8,64,512]{2,1,0:T(8,128)(2,1)}, u32[]{:S(2)}, u32[]{:S(2)}) collective-permute-start(bf16[8,64,512]{2,1,0:T(8,128)(2,1)} %get-tuple-element.13), channel_id=1, source_target_pairs={{0,16},{16,0},{1,17},{17,1},{2,18},{18,2},{3,19},{19,3},{4,20},{20... | collective-permute-start | bytes 1572872 | tf_op jit(solution)/shard_map/ppermute | solution.py:269
  97.7 2.6 %collective-permute-start.3 = (bf16[8,64,512]{2,1,0:T(8,128)(2,1)}, bf16[8,64,512]{2,1,0:T(8,128)(2,1)}, u32[]{:S(2)}, u32[]{:S(2)}) collective-permute-start(bf16[8,64,512]{2,1,0:T(8,128)(2,1)} %get-tuple-element.14), channel_id=1, source_target_pairs={{0,16},{16,0},{1,17},{17,1},{2,18},{18,2},{3,19},{19,3},{4,20},{20... | collective-permute-start | bytes 1572872 | tf_op jit(solution)/shard_map/ppermute | solution.py:269
  98.6 3.0 %copy-start.2 = (bf16[16,128,512]{2,1,0:T(8,128)(2,1)S(1)}, bf16[16,128,512]{2,1,0:T(8,128)(2,1)}, u32[]{:S(2)}) copy-start(bf16[16,128,512]{2,1,0:T(8,128)(2,1)} %weight_ref.1) | copy-start | bytes 6291460
  101.6 13.8 %copy-start = (bf16[384,2048]{1,0:T(8,128)(2,1)S(1)}, bf16[384,2048]{1,0:T(8,128)(2,1)}, u32[]{:S(2)}) copy-start(bf16[384,2048]{1,0:T(8,128)(2,1)} %tokens_ref.1) | copy-start | bytes 4718596

commit v4 on v3

--- a/solution.py
+++ b/solution.py
@@ -31,30 +31,46 @@
         out_ref[some] = held[some].astype(bf16)
 
 
-def orthogonalize(x_ref, out_ref, held, staged, sems):
-    rows = x_ref.shape[0]
+def cross(left, right):
+    return lax.dot_general(left, right, (((0,), (0,)), ((), ())), preferred_element_type=f32)
+
+
+def trace(block):
+    diagonal = lax.broadcasted_iota(jnp.int32, block.shape, 0) == lax.broadcasted_iota(
+        jnp.int32, block.shape, 1
+    )
+    total = jnp.sum(jnp.where(diagonal, block, 0.0), axis=0, keepdims=True)
+    return jnp.sum(total, axis=1, keepdims=True)
+
+
+def orthogonalize(x_ref, out_ref, gram_ref, held, staged, sems):
+    rows, width = x_ref.shape
+    low, high = slice(0, width // 2), slice(width // 2, width)
     copies = []
-    step = rows // 4
     scale = None
     for turn in range(ITERS):
         source = x_ref if turn == 0 else held
-        x = source[...]
-        gram = lax.dot_general(x, x, (((0,), (0,)), ((), ())), preferred_element_type=f32)
+        left, right = source[:, low], source[:, high]
+        upper = cross(left, right)
         if turn == 0:
-            diagonal = lax.broadcasted_iota(jnp.int32, gram.shape, 0) == lax.broadcasted_iota(
-                jnp.int32, gram.shape, 1
-            )
-            norm2 = jnp.sum(
-                jnp.sum(jnp.where(diagonal, gram, 0.0), axis=0, keepdims=True),
-                axis=1,
-                keepdims=True,
-            )
+            first, last = cross(left, left), cross(right, right)
+            norm2 = trace(first) + trace(last)
             scale = 1.0 / (jnp.sqrt(norm2) + 1e-07)
-            gram = jnp.where(norm2 < jnp.inf, gram * scale * scale, 0.0)
-        g = gram.astype(bf16)
+
+            def scaled(block):
+                return jnp.where(norm2 < jnp.inf, block * scale * scale, 0.0)
+
+            upper, first, last = scaled(upper), scaled(first), scaled(last)
+        gram_ref[low, high] = upper.astype(bf16)
+        gram_ref[high, low] = upper.T.astype(bf16)
+        gram_ref[low, low] = (first if turn == 0 else cross(left, left)).astype(bf16)
+        gram_ref[high, high] = (last if turn == 0 else cross(right, right)).astype(bf16)
+        g = gram_ref[...]
         square = jnp.dot(g, g, preferred_element_type=f32)
         poly = (coef_b * g.astype(f32) + coef_c * square).astype(bf16)
-        for part in range(4):
+        parts = 4 if turn < ITERS - 1 else sems.shape[0]
+        step = rows // parts
+        for part in range(parts):
             at = pl.ds(part * step, step)
             piece = source[at, :]
             fresh = coef_a * piece.astype(f32) + jnp.dot(piece, poly, preferred_element_type=f32)
@@ -230,9 +246,10 @@
         in_specs=[vmem],
         out_specs=hbm,
         scratch_shapes=[
+            pltpu.VMEM((width, width), bf16),
             pltpu.VMEM((ranks * rows, width), bf16),
             pltpu.VMEM((ranks * rows, width), bf16),
-            pltpu.SemaphoreType.DMA((4,)),
+            pltpu.SemaphoreType.DMA((8,)),
         ],
         compiler_params=params,
         name="orthogonalize",

time: 117 us -> 117 us (level)
  no operation moved by 1% of the time
where the time goes in v4:
time: 117 us; the launch traced here: 116 us
  blocking collectives  35.6 us (30%)
  waiting for transfers between devices  33.9 us (29%)
  Pallas kernels  24.6 us (21%)
  starting transfers between devices  14.8 us (13%)
  other arithmetic  5.68 us (5%)
  between operations  1.41 us (1%)
    all_to_all x1, blocking collectives, exchange(): return lax.all_to_all(data, axes, split_axis=0, concat_axis=0, tiled=True)  35.6 us
    all_to_all x2, waiting for transfers between devices, exchange(): return lax.all_to_all(data, axes, split_axis=0, concat_axis=0, tiled=True)  29.9 us
    pallas_call x1, Pallas kernels, body(): pl.pallas_call(orthogonalize, out_shape=pltpu.HBM((ranks * rows, width),...  13.7 us
    all_to_all x2, starting transfers between devices, exchange(): return lax.all_to_all(data, axes, split_axis=0, concat_axis=0, tiled=True)  13 us
    pallas_call x1, Pallas kernels, body(): pl.pallas_call(gather_old, out_shape=(pltpu.HBM((ranks, half, width), bf1...  4.44 us
    convert_element_type x1, other arithmetic, body(): new = new.astype(bf16).reshape(weight.shape)  2.83 us
    pallas_call x1, Pallas kernels, body(): pl.pallas_call(combine, out_shape=(pltpu.HBM((ranks, 2 * planes, lanes, 1...  2.79 us
    ppermute x1, waiting for transfers between devices, body(): theirs = lax.ppermute(theirs, 'core', swap)  2.36 us
  transfers between devices with their start and end apart: 6, of which 5 were waited for; matrix products, arithmetic and copies ran while one was open for 5% of the time, Pallas kernels for 4%

profile of v4, /device:TPU:1, one launch (start us, length us, event | category | flops | bytes accessed | tf_op | source)
XLA Modules:
  0.0 116.2 jit_solution(7264128939082147338)
XLA Ops:
  0.6 2.3 %narrow.1 = bf16[16,128,512]{2,1,0:T(8,128)(2,1)S(1)} custom-call(f32[16,128,512]{2,1,0:T(8,128)} %far_ref.1), custom_call_target="tpu_custom_call" | custom-call | tf_op jit(solution)/shard_map/narrow/pallas_call | solution.py:209
  2.9 35.6 %all_to_all.15 = bf16[16,128,512]{2,1,0:T(8,128)(2,1)S(1)} all-to-all(bf16[16,128,512]{2,1,0:T(8,128)(2,1)S(1)} %narrow.1), channel_id=1, replica_groups=mesh['y'=4,'core'=2,'row'=16] {'row'}, dimensions={0} | all-to-all | bytes 4194304 | tf_op jit(solution)/shard_map/all_to_all | solution.py:207
  38.5 13.7 %orthogonalize.1 = bf16[2048,512]{1,0:T(8,128)(2,1)} custom-call(bf16[2048,512]{1,0:T(8,128)(2,1)S(1)} %bitcast.18), custom_call_target="tpu_custom_call" | custom-call | tf_op jit(solution)/shard_map/orthogonalize/pallas_call | solution.py:243
  52.2 0.0 copy-start.1
  52.2 5.8 %all-to-all-start.1 = ((bf16[32,64,512]{2,1,0:T(8,128)(2,1)}), bf16[32,64,512]{2,1,0:T(8,128)(2,1)S(1)}, u32[]{:S(2)}, u32[]{:S(2)}) async-start(bf16[32,64,512]{2,1,0:T(8,128)(2,1)} %bitcast.21), calls=%async_computation.1 | async-start | bytes 4194304 | tf_op jit(solution)/shard_map/all_to_all | solution.py:207
  58.1 4.4 %gather_old.1 = (bf16[16,64,512]{2,1,0:T(8,128)(2,1)}, bf16[16,64,512]{2,1,0:T(8,128)(2,1)}, s32[2,16]{1,0:T(2,128)S(1)}) custom-call(s32[16]{0:T(128)S(1)} %bitcast.20, s32[1]{0:T(128)} %bitcast.6.core_ref, bf16[16,128,512]{2,1,0:T(8,128)(2,1)} %weight_ref.1), custom_call_target="tpu_custom_call" | custom-call | tf_op jit(solution)/shard_map/gather_old/pallas_call | solution.py:221
  62.5 0.4 collective-permute-start.1
  63.0 0.2 collective-permute-start
  63.1 2.4 %collective-permute-done.1 = bf16[16,64,512]{2,1,0:T(8,128)(2,1)S(1)} collective-permute-done((bf16[16,64,512]{2,1,0:T(8,128)(2,1)}, bf16[16,64,512]{2,1,0:T(8,128)(2,1)S(1)}, u32[]{:S(2)}, u32[]{:S(2)}) %collective-permute-start.1) | collective-permute-done | bytes 1048608 | tf_op jit(solution)/shard_map/ppermute | solution.py:239
  65.5 1.5 %add_convert_fusion.old_ref = bf16[16,64,512]{2,1,0:T(8,128)(2,1)S(1)} fusion(bf16[16,64,512]{2,1,0:T(8,128)(2,1)S(1)} %collective-permute-done.1, bf16[16,64,512]{2,1,0:T(8,128)(2,1)} %get-tuple-element.11), kind=kLoop, calls=%fused_computation.2 | loop fusion | flops 2097152 | bytes 3145728 | tf_op jit(solution)/shard_map/convert_element_type | solution.py:241
  67.1 19.0 %all-to-all-done.1 = bf16[32,64,512]{2,1,0:T(8,128)(2,1)S(1)} async-done(((bf16[32,64,512]{2,1,0:T(8,128)(2,1)}), bf16[32,64,512]{2,1,0:T(8,128)(2,1)S(1)}, u32[]{:S(2)}, u32[]{:S(2)}) %all-to-all-start.1) | async-done | bytes 2097184 | tf_op jit(solution)/shard_map/all_to_all | solution.py:207
  86.0 2.8 %combine.1 = (bf16[16,8,32,128]{3,2,1,0:T(8,128)(2,1)}, bf16[8,64,512]{2,1,0:T(8,128)(2,1)}, bf16[8,64,512]{2,1,0:T(8,128)(2,1)}) custom-call(s32[2,16]{1,0:T(2,128)S(1)} %get-tuple-element.10.table_ref, s32[2,16]{1,0:T(2,128)S(1)} %collective-permute-done.pair_ref, s32[1]{0:T(128)} %bitcast.6.core_ref, bf16[16,64,512]{2,1,0:T(8,128)(2,1)S(1)} %add_convert_fusion.old_ref, ...), custom_call_target="tpu_custom_call" | custom-call | tf_op jit(solution)/shard_map/combine/pallas_call | solution.py:261
  88.8 7.1 %all-to-all-start.2 = ((bf16[128,32,128]{2,1,0:T(8,128)(2,1)}), bf16[128,32,128]{2,1,0:T(8,128)(2,1)S(1)}, u32[]{:S(2)}, u32[]{:S(2)}) async-start(bf16[128,32,128]{2,1,0:T(8,128)(2,1)} %bitcast.22), calls=%async_computation.2 | async-start | bytes 2097152 | tf_op jit(solution)/shard_map/all_to_all | solution.py:207
  96.0 1.1 collective-permute-start.2
  97.1 0.1 collective-permute-start.3
  97.2 0.1 broadcast_in_dim.38
  97.3 0.1 broadcast_in_dim.39
  98.0 0.1 dynamic-slice_bitcast_fusion
  98.1 0.9 collective-permute-done.2
  99.0 0.7 collective-permute-done.3
  99.7 1.3 %pad_maximum_fusion = bf16[16,64,512]{2,1,0:T(8,128)(2,1)S(1)} fusion(bf16[8,64,512]{2,1,0:T(8,128)(2,1)} %collective-permute-done.3, bf16[8,64,512]{2,1,0:T(8,128)(2,1)} %collective-permute-done.2), kind=kLoop, calls=%fused_computation.3 | loop fusion | flops 524288 | bytes 2097152 | tf_op jit(solution)/shard_map/concatenate | solution.py:286
  101.1 2.8 %subtract_convert_fusion = bf16[16,128,512]{2,1,0:T(8,128)(2,1)} fusion(bf16[16,128,512]{2,1,0:T(8,128)(2,1)S(1)} %copy-done.2, pred[128]{0:T(512)(128)(4,1)S(1)} %broadcast_in_dim.39, bf16[16,64,512]{2,1,0:T(8,128)(2,1)S(1)} %pad_maximum_fusion, bf16[16,64,512]{2,1,0:T(8,128)(2,1)S(1)} %dynamic-slice_bitcast_fusion), kind=kLoop, calls=%fused_computation | loop fusion | flops 6291456 | bytes 6291584 | tf_op jit(solution)/shard_map/convert_element_type | solution.py:291
  103.9 11.0 %all-to-all-done.2 = bf16[128,32,128]{2,1,0:T(8,128)(2,1)S(1)} async-done(((bf16[128,32,128]{2,1,0:T(8,128)(2,1)}), bf16[128,32,128]{2,1,0:T(8,128)(2,1)S(1)}, u32[]{:S(2)}, u32[]{:S(2)}) %all-to-all-start.2) | async-done | bytes 1048608 | tf_op jit(solution)/shard_map/all_to_all | solution.py:207
  114.9 1.4 %project.1 = bf16[64,384]{1,0:T(8,128)(2,1)} custom-call(s32[1]{0:T(128)S(6)} %copy.7.count_ref, s32[1]{0:T(128)} %bitcast.6.core_ref, bf16[384,2048]{1,0:T(8,128)(2,1)S(1)} %copy-done, bf16[16,4,2,32,128]{4,3,2,1,0:T(8,128)(2,1)S(1)} %bitcast.19), custom_call_target="tpu_custom_call" | custom-call | tf_op jit(solution)/shard_map/project/pallas_call | solution.py:293
  (7 shorter events, 0.0 us)
Async XLA Ops:
  52.2 5.9 %copy-start.1 = (s32[16,1]{0,1:T(1,128)S(1)}, s32[16,1]{0,1:T(1,128)}, u32[]{:S(2)}) copy-start(s32[16,1]{0,1:T(1,128)} %param.7) | copy-start | bytes 196
  52.2 33.8 %all-to-all-start.1 = ((bf16[32,64,512]{2,1,0:T(8,128)(2,1)}), bf16[32,64,512]{2,1,0:T(8,128)(2,1)S(1)}, u32[]{:S(2)}, u32[]{:S(2)}) async-start(bf16[32,64,512]{2,1,0:T(8,128)(2,1)} %bitcast.21), calls=%async_computation.1 | async-start | bytes 4194304 | tf_op jit(solution)/shard_map/all_to_all | solution.py:207
  62.5 3.0 %collective-permute-start.1 = (bf16[16,64,512]{2,1,0:T(8,128)(2,1)}, bf16[16,64,512]{2,1,0:T(8,128)(2,1)S(1)}, u32[]{:S(2)}, u32[]{:S(2)}) collective-permute-start(bf16[16,64,512]{2,1,0:T(8,128)(2,1)} %get-tuple-element.12), channel_id=1, source_target_pairs={{0,16},{16,0},{1,17},{17,1},{2,18},{18,2},{3,19},{19,3},{4,20},{20... | collective-permute-start | bytes 3145736 | tf_op jit(solution)/shard_map/ppermute | solution.py:239
  63.0 4.1 %collective-permute-start = (s32[2,16]{1,0:T(2,128)S(1)}, s32[2,16]{1,0:T(2,128)S(1)}, u32[]{:S(2)}, u32[]{:S(2)}) collective-permute-start(s32[2,16]{1,0:T(2,128)S(1)} %get-tuple-element.10.table_ref), channel_id=1, source_target_pairs={{0,16},{16,0},{1,17},{17,1},{2,18},{18,2},{3,19},{19,3},{4,20},{20... | collective-permute-start | bytes 392 | tf_op jit(solution)/shard_map/ppermute | solution.py:240
  88.8 26.1 %all-to-all-start.2 = ((bf16[128,32,128]{2,1,0:T(8,128)(2,1)}), bf16[128,32,128]{2,1,0:T(8,128)(2,1)S(1)}, u32[]{:S(2)}, u32[]{:S(2)}) async-start(bf16[128,32,128]{2,1,0:T(8,128)(2,1)} %bitcast.22), calls=%async_computation.2 | async-start | bytes 2097152 | tf_op jit(solution)/shard_map/all_to_all | solution.py:207
  96.0 3.0 %collective-permute-start.2 = (bf16[8,64,512]{2,1,0:T(8,128)(2,1)}, bf16[8,64,512]{2,1,0:T(8,128)(2,1)}, u32[]{:S(2)}, u32[]{:S(2)}) collective-permute-start(bf16[8,64,512]{2,1,0:T(8,128)(2,1)} %get-tuple-element.13), channel_id=1, source_target_pairs={{0,16},{16,0},{1,17},{17,1},{2,18},{18,2},{3,19},{19,3},{4,20},{20... | collective-permute-start | bytes 1572872 | tf_op jit(solution)/shard_map/ppermute | solution.py:286
  97.1 2.6 %collective-permute-start.3 = (bf16[8,64,512]{2,1,0:T(8,128)(2,1)}, bf16[8,64,512]{2,1,0:T(8,128)(2,1)}, u32[]{:S(2)}, u32[]{:S(2)}) collective-permute-start(bf16[8,64,512]{2,1,0:T(8,128)(2,1)} %get-tuple-element.14), channel_id=1, source_target_pairs={{0,16},{16,0},{1,17},{17,1},{2,18},{18,2},{3,19},{19,3},{4,20},{20... | collective-permute-start | bytes 1572872 | tf_op jit(solution)/shard_map/ppermute | solution.py:286
  98.0 3.0 %copy-start.2 = (bf16[16,128,512]{2,1,0:T(8,128)(2,1)S(1)}, bf16[16,128,512]{2,1,0:T(8,128)(2,1)}, u32[]{:S(2)}) copy-start(bf16[16,128,512]{2,1,0:T(8,128)(2,1)} %weight_ref.1) | copy-start | bytes 6291460
  101.0 13.8 %copy-start = (bf16[384,2048]{1,0:T(8,128)(2,1)S(1)}, bf16[384,2048]{1,0:T(8,128)(2,1)}, u32[]{:S(2)}) copy-start(bf16[384,2048]{1,0:T(8,128)(2,1)} %tokens_ref.1) | copy-start | bytes 4718596

commit v5 on v4

--- a/solution.py
+++ b/solution.py
@@ -192,7 +192,7 @@
 
 def body(grad, weight, owner, tokens, counts):
     number, rows, width = grad.shape
-    ranks = lax.axis_size("row")
+    ranks = lax.axis_size("z") * lax.axis_size("x")
     planes = lax.axis_size("y")
     half = rows // 2
     index = lax.axis_index("core")
@@ -215,7 +215,7 @@
         compiler_params=params,
         name="narrow",
     )(pltpu.with_memory_space_constraint(grad, pltpu.HBM))
-    whole = exchange(narrowed, "row")
+    whole = exchange(narrowed, ("x", "z"))
 
     named = owner[:, 0]
     mine, theirs, table = pl.pallas_call(
@@ -254,7 +254,7 @@
         compiler_params=params,
         name="orthogonalize",
     )(whole.reshape(ranks * rows, width))
-    back = exchange(ortho.reshape(2 * ranks, half, width), ("row", "core"))
+    back = exchange(ortho.reshape(2 * ranks, half, width), ("x", "z", "core"))
     back = back.reshape(number, 2, half, width)
 
     lanes = half // 2
@@ -280,7 +280,7 @@
         old,
         back,
     )
-    sums = exchange(sums.reshape(-1, lanes, 128), ("row", "y", "core"))
+    sums = exchange(sums.reshape(-1, lanes, 128), ("z", "x", "y", "core"))
     sums = sums.reshape(ranks, planes, 2, lanes, 128)
 
     other = jnp.concatenate([lax.ppermute(piece, "core", swap) for piece in passed])
@@ -303,19 +303,20 @@
 
 
 def solution(mesh):
-    devices = mesh.devices.reshape(mesh.shape["grp"] // 2, 2, mesh.shape["row"])
-    inner = Mesh(devices, ("y", "core", "row"))
-    group = ("y", "core")
+    side = round(mesh.shape["row"] ** 0.5)
+    devices = mesh.devices.reshape(mesh.shape["grp"] // 2, 2, side, side)
+    inner = Mesh(devices, ("y", "core", "z", "x"))
+    group, row = ("y", "core"), ("z", "x")
     return jax.shard_map(
         body,
         mesh=inner,
         in_specs=(
-            P(group, "row", None),
-            P(group, "row", None),
+            P(group, row, None),
+            P(group, row, None),
             P(group, None),
-            P("row", None),
-            P("row"),
+            P(row, None),
+            P(row),
         ),
-        out_specs=(P(group, "row", None), P("row", group)),
+        out_specs=(P(group, row, None), P(row, group)),
         check_vma=False,
     )

time: 117 us -> 116 us (level)
  no operation moved by 1% of the time
where the time goes in v5:
time: 116 us; the launch traced here: 115 us
  blocking collectives  34.7 us (30%)
  waiting for transfers between devices  34.3 us (30%)
  Pallas kernels  24.6 us (21%)
  starting transfers between devices  14.4 us (12%)
  other arithmetic  5.68 us (5%)
  between operations  1.41 us (1%)
    all_to_all x1, blocking collectives, exchange(): return lax.all_to_all(data, axes, split_axis=0, concat_axis=0, tiled=True)  34.7 us
    all_to_all x2, waiting for transfers between devices, exchange(): return lax.all_to_all(data, axes, split_axis=0, concat_axis=0, tiled=True)  30.3 us
    pallas_call x1, Pallas kernels, body(): pl.pallas_call(orthogonalize, out_shape=pltpu.HBM((ranks * rows, width),...  13.7 us
    all_to_all x2, starting transfers between devices, exchange(): return lax.all_to_all(data, axes, split_axis=0, concat_axis=0, tiled=True)  12.5 us
    pallas_call x1, Pallas kernels, body(): pl.pallas_call(gather_old, out_shape=(pltpu.HBM((ranks, half, width), bf1...  4.44 us
    convert_element_type x1, other arithmetic, body(): new = new.astype(bf16).reshape(weight.shape)  2.83 us
    pallas_call x1, Pallas kernels, body(): pl.pallas_call(combine, out_shape=(pltpu.HBM((ranks, 2 * planes, lanes, 1...  2.79 us
    ppermute x1, waiting for transfers between devices, body(): theirs = lax.ppermute(theirs, 'core', swap)  2.36 us
  transfers between devices with their start and end apart: 6, of which 5 were waited for; matrix products, arithmetic and copies ran while one was open for 5% of the time, Pallas kernels for 4%

profile of v5, /device:TPU:1, one launch (start us, length us, event | category | flops | bytes accessed | tf_op | source)
XLA Modules:
  0.0 115.3 jit_solution(11750957408783207515)
XLA Ops:
  0.6 2.3 %narrow.1 = bf16[16,128,512]{2,1,0:T(8,128)(2,1)S(1)} custom-call(f32[16,128,512]{2,1,0:T(8,128)} %far_ref.1), custom_call_target="tpu_custom_call" | custom-call | tf_op jit(solution)/shard_map/narrow/pallas_call | solution.py:209
  2.9 34.7 %all_to_all.15 = bf16[16,128,512]{2,1,0:T(8,128)(2,1)S(1)} all-to-all(bf16[16,128,512]{2,1,0:T(8,128)(2,1)S(1)} %narrow.1), channel_id=1, replica_groups=mesh['y'=4,'core'=2,'z'=4,'x'=4] {'x','z'}, dimensions={0} | all-to-all | bytes 4194304 | tf_op jit(solution)/shard_map/all_to_all | solution.py:207
  37.7 13.7 %orthogonalize.1 = bf16[2048,512]{1,0:T(8,128)(2,1)} custom-call(bf16[2048,512]{1,0:T(8,128)(2,1)S(1)} %bitcast.18), custom_call_target="tpu_custom_call" | custom-call | tf_op jit(solution)/shard_map/orthogonalize/pallas_call | solution.py:243
  51.4 0.0 copy-start.1
  51.4 6.6 %all-to-all-start.1 = ((bf16[32,64,512]{2,1,0:T(8,128)(2,1)}), bf16[32,64,512]{2,1,0:T(8,128)(2,1)S(1)}, u32[]{:S(2)}, u32[]{:S(2)}) async-start(bf16[32,64,512]{2,1,0:T(8,128)(2,1)} %bitcast.21), calls=%async_computation.1 | async-start | bytes 4194304 | tf_op jit(solution)/shard_map/all_to_all | solution.py:207
  58.0 4.4 %gather_old.1 = (bf16[16,64,512]{2,1,0:T(8,128)(2,1)}, bf16[16,64,512]{2,1,0:T(8,128)(2,1)}, s32[2,16]{1,0:T(2,128)S(1)}) custom-call(s32[16]{0:T(128)S(1)} %bitcast.20, s32[1]{0:T(128)} %bitcast.6.core_ref, bf16[16,128,512]{2,1,0:T(8,128)(2,1)} %weight_ref.1), custom_call_target="tpu_custom_call" | custom-call | tf_op jit(solution)/shard_map/gather_old/pallas_call | solution.py:221
  62.5 0.4 collective-permute-start.1
  62.8 0.2 collective-permute-start
  63.0 2.4 %collective-permute-done.1 = bf16[16,64,512]{2,1,0:T(8,128)(2,1)S(1)} collective-permute-done((bf16[16,64,512]{2,1,0:T(8,128)(2,1)}, bf16[16,64,512]{2,1,0:T(8,128)(2,1)S(1)}, u32[]{:S(2)}, u32[]{:S(2)}) %collective-permute-start.1) | collective-permute-done | bytes 1048608 | tf_op jit(solution)/shard_map/ppermute | solution.py:239
  65.4 1.5 %add_convert_fusion.old_ref = bf16[16,64,512]{2,1,0:T(8,128)(2,1)S(1)} fusion(bf16[16,64,512]{2,1,0:T(8,128)(2,1)S(1)} %collective-permute-done.1, bf16[16,64,512]{2,1,0:T(8,128)(2,1)} %get-tuple-element.11), kind=kLoop, calls=%fused_computation.2 | loop fusion | flops 2097152 | bytes 3145728 | tf_op jit(solution)/shard_map/convert_element_type | solution.py:241
  67.0 19.3 %all-to-all-done.1 = bf16[32,64,512]{2,1,0:T(8,128)(2,1)S(1)} async-done(((bf16[32,64,512]{2,1,0:T(8,128)(2,1)}), bf16[32,64,512]{2,1,0:T(8,128)(2,1)S(1)}, u32[]{:S(2)}, u32[]{:S(2)}) %all-to-all-start.1) | async-done | bytes 2097184 | tf_op jit(solution)/shard_map/all_to_all | solution.py:207
  86.3 2.8 %combine.1 = (bf16[16,8,32,128]{3,2,1,0:T(8,128)(2,1)}, bf16[8,64,512]{2,1,0:T(8,128)(2,1)}, bf16[8,64,512]{2,1,0:T(8,128)(2,1)}) custom-call(s32[2,16]{1,0:T(2,128)S(1)} %get-tuple-element.10.table_ref, s32[2,16]{1,0:T(2,128)S(1)} %collective-permute-done.pair_ref, s32[1]{0:T(128)} %bitcast.6.core_ref, bf16[16,64,512]{2,1,0:T(8,128)(2,1)S(1)} %add_convert_fusion.old_ref, ...), custom_call_target="tpu_custom_call" | custom-call | tf_op jit(solution)/shard_map/combine/pallas_call | solution.py:261
  89.1 5.9 %all-to-all-start.2 = ((bf16[128,32,128]{2,1,0:T(8,128)(2,1)}), bf16[128,32,128]{2,1,0:T(8,128)(2,1)S(1)}, u32[]{:S(2)}, u32[]{:S(2)}) async-start(bf16[128,32,128]{2,1,0:T(8,128)(2,1)} %bitcast.22), calls=%async_computation.2 | async-start | bytes 2097152 | tf_op jit(solution)/shard_map/all_to_all | solution.py:207
  95.0 1.1 collective-permute-start.2
  96.2 0.1 collective-permute-start.3
  96.3 0.1 broadcast_in_dim.38
  96.3 0.1 broadcast_in_dim.39
  97.1 0.1 dynamic-slice_bitcast_fusion
  97.2 0.9 collective-permute-done.2
  98.0 0.7 collective-permute-done.3
  98.8 1.3 %pad_maximum_fusion = bf16[16,64,512]{2,1,0:T(8,128)(2,1)S(1)} fusion(bf16[8,64,512]{2,1,0:T(8,128)(2,1)} %collective-permute-done.3, bf16[8,64,512]{2,1,0:T(8,128)(2,1)} %collective-permute-done.2), kind=kLoop, calls=%fused_computation.3 | loop fusion | flops 524288 | bytes 2097152 | tf_op jit(solution)/shard_map/concatenate | solution.py:286
  100.1 2.8 %subtract_convert_fusion = bf16[16,128,512]{2,1,0:T(8,128)(2,1)} fusion(bf16[16,128,512]{2,1,0:T(8,128)(2,1)S(1)} %copy-done.2, pred[128]{0:T(512)(128)(4,1)S(1)} %broadcast_in_dim.39, bf16[16,64,512]{2,1,0:T(8,128)(2,1)S(1)} %pad_maximum_fusion, bf16[16,64,512]{2,1,0:T(8,128)(2,1)S(1)} %dynamic-slice_bitcast_fusion), kind=kLoop, calls=%fused_computation | loop fusion | flops 6291456 | bytes 6291584 | tf_op jit(solution)/shard_map/convert_element_type | solution.py:291
  102.9 11.0 %all-to-all-done.2 = bf16[128,32,128]{2,1,0:T(8,128)(2,1)S(1)} async-done(((bf16[128,32,128]{2,1,0:T(8,128)(2,1)}), bf16[128,32,128]{2,1,0:T(8,128)(2,1)S(1)}, u32[]{:S(2)}, u32[]{:S(2)}) %all-to-all-start.2) | async-done | bytes 1048608 | tf_op jit(solution)/shard_map/all_to_all | solution.py:207
  113.9 1.4 %project.1 = bf16[64,384]{1,0:T(8,128)(2,1)} custom-call(s32[1]{0:T(128)S(6)} %copy.7.count_ref, s32[1]{0:T(128)} %bitcast.6.core_ref, bf16[384,2048]{1,0:T(8,128)(2,1)S(1)} %copy-done, bf16[16,4,2,32,128]{4,3,2,1,0:T(8,128)(2,1)S(1)} %bitcast.19), custom_call_target="tpu_custom_call" | custom-call | tf_op jit(solution)/shard_map/project/pallas_call | solution.py:293
  (7 shorter events, 0.0 us)
Async XLA Ops:
  51.4 6.6 %copy-start.1 = (s32[16,1]{0,1:T(1,128)S(1)}, s32[16,1]{0,1:T(1,128)}, u32[]{:S(2)}) copy-start(s32[16,1]{0,1:T(1,128)} %param.7) | copy-start | bytes 196
  51.4 34.9 %all-to-all-start.1 = ((bf16[32,64,512]{2,1,0:T(8,128)(2,1)}), bf16[32,64,512]{2,1,0:T(8,128)(2,1)S(1)}, u32[]{:S(2)}, u32[]{:S(2)}) async-start(bf16[32,64,512]{2,1,0:T(8,128)(2,1)} %bitcast.21), calls=%async_computation.1 | async-start | bytes 4194304 | tf_op jit(solution)/shard_map/all_to_all | solution.py:207
  62.5 3.0 %collective-permute-start.1 = (bf16[16,64,512]{2,1,0:T(8,128)(2,1)}, bf16[16,64,512]{2,1,0:T(8,128)(2,1)S(1)}, u32[]{:S(2)}, u32[]{:S(2)}) collective-permute-start(bf16[16,64,512]{2,1,0:T(8,128)(2,1)} %get-tuple-element.12), channel_id=1, source_target_pairs={{0,16},{16,0},{1,17},{17,1},{2,18},{18,2},{3,19},{19,3},{4,20},{20... | collective-permute-start | bytes 3145736 | tf_op jit(solution)/shard_map/ppermute | solution.py:239
  62.8 4.1 %collective-permute-start = (s32[2,16]{1,0:T(2,128)S(1)}, s32[2,16]{1,0:T(2,128)S(1)}, u32[]{:S(2)}, u32[]{:S(2)}) collective-permute-start(s32[2,16]{1,0:T(2,128)S(1)} %get-tuple-element.10.table_ref), channel_id=1, source_target_pairs={{0,16},{16,0},{1,17},{17,1},{2,18},{18,2},{3,19},{19,3},{4,20},{20... | collective-permute-start | bytes 392 | tf_op jit(solution)/shard_map/ppermute | solution.py:240
  89.1 24.8 %all-to-all-start.2 = ((bf16[128,32,128]{2,1,0:T(8,128)(2,1)}), bf16[128,32,128]{2,1,0:T(8,128)(2,1)S(1)}, u32[]{:S(2)}, u32[]{:S(2)}) async-start(bf16[128,32,128]{2,1,0:T(8,128)(2,1)} %bitcast.22), calls=%async_computation.2 | async-start | bytes 2097152 | tf_op jit(solution)/shard_map/all_to_all | solution.py:207
  95.0 3.0 %collective-permute-start.2 = (bf16[8,64,512]{2,1,0:T(8,128)(2,1)}, bf16[8,64,512]{2,1,0:T(8,128)(2,1)}, u32[]{:S(2)}, u32[]{:S(2)}) collective-permute-start(bf16[8,64,512]{2,1,0:T(8,128)(2,1)} %get-tuple-element.13), channel_id=1, source_target_pairs={{0,16},{16,0},{1,17},{17,1},{2,18},{18,2},{3,19},{19,3},{4,20},{20... | collective-permute-start | bytes 1572872 | tf_op jit(solution)/shard_map/ppermute | solution.py:286
  96.2 2.6 %collective-permute-start.3 = (bf16[8,64,512]{2,1,0:T(8,128)(2,1)}, bf16[8,64,512]{2,1,0:T(8,128)(2,1)}, u32[]{:S(2)}, u32[]{:S(2)}) collective-permute-start(bf16[8,64,512]{2,1,0:T(8,128)(2,1)} %get-tuple-element.14), channel_id=1, source_target_pairs={{0,16},{16,0},{1,17},{17,1},{2,18},{18,2},{3,19},{19,3},{4,20},{20... | collective-permute-start | bytes 1572872 | tf_op jit(solution)/shard_map/ppermute | solution.py:286
  97.1 3.0 %copy-start.2 = (bf16[16,128,512]{2,1,0:T(8,128)(2,1)S(1)}, bf16[16,128,512]{2,1,0:T(8,128)(2,1)}, u32[]{:S(2)}) copy-start(bf16[16,128,512]{2,1,0:T(8,128)(2,1)} %weight_ref.1) | copy-start | bytes 6291460
  100.1 13.8 %copy-start = (bf16[384,2048]{1,0:T(8,128)(2,1)S(1)}, bf16[384,2048]{1,0:T(8,128)(2,1)}, u32[]{:S(2)}) copy-start(bf16[384,2048]{1,0:T(8,128)(2,1)} %tokens_ref.1) | copy-start | bytes 4718596

commit v6 on v5

--- a/solution.py
+++ b/solution.py
@@ -145,7 +145,8 @@
         passing[-1].start()
     low = lax.broadcasted_iota(jnp.int32, (lanes, 128), 1) < 64
     copies = []
-    for r in range(number):
+    for k in range(number):
+        r = k % 4 * 4 + k // 4
         slots = []
         for slot in range(4):
             e = (table_ref if slot < 2 else pair_ref)[slot % 2, r]
@@ -160,12 +161,12 @@
             total = old_ref[r, :, columns].astype(f32) - step_size * move
             top = total[:lanes]
             bottom = pltpu.roll(total[lanes:], 64, 1)
-            staged[r, 2 * t] = jnp.where(low, top, bottom).astype(bf16)
-            staged[r, 2 * t + 1] = jnp.where(low, bottom, top).astype(bf16)
-        if r % 2 == 1:
-            ready = pl.ds(r - 1, 2)
+            staged[k, 2 * t] = jnp.where(low, top, bottom).astype(bf16)
+            staged[k, 2 * t + 1] = jnp.where(low, bottom, top).astype(bf16)
+        if k % 2 == 1:
+            ready = pl.ds(k - 1, 2)
             copies.append(
-                pltpu.make_async_copy(staged.at[ready], sum_ref.at[ready], sems.at[r // 2])
+                pltpu.make_async_copy(staged.at[ready], sum_ref.at[ready], sems.at[k // 2])
             )
             copies[-1].start()
     for copy in copies:
@@ -176,12 +177,13 @@
 
 def project(count_ref, core_ref, tokens_ref, sums_ref, out_ref, held):
     ranks, planes, halves, rows, _ = sums_ref.shape
-    for r in range(ranks):
+    for k in range(ranks):
+        r = k % 4 * 4 + k // 4
         for h in range(halves):
             first = (2 * r + h) * 2 * rows
-            total = sums_ref[r, 0, h].astype(f32)
+            total = sums_ref[k, 0, h].astype(f32)
             for y in range(1, planes):
-                total = total + sums_ref[r, y, h].astype(f32)
+                total = total + sums_ref[k, y, h].astype(f32)
             held[first : first + rows, :] = total.astype(bf16)
             held[first + rows : first + 2 * rows, :] = pltpu.roll(total, 64, 1).astype(bf16)
     full = jnp.dot(tokens_ref[...], held[...], preferred_element_type=f32).T
@@ -280,7 +282,7 @@
         old,
         back,
     )
-    sums = exchange(sums.reshape(-1, lanes, 128), ("z", "x", "y", "core"))
+    sums = exchange(sums.reshape(-1, lanes, 128), ("x", "z", "y", "core"))
     sums = sums.reshape(ranks, planes, 2, lanes, 128)
 
     other = jnp.concatenate([lax.ppermute(piece, "core", swap) for piece in passed])

time: 116 us -> 116 us (level)
  no operation moved by 1% of the time
where the time goes in v6:
time: 116 us; the launch traced here: 115 us
  blocking collectives  34.7 us (30%)
  waiting for transfers between devices  34.5 us (30%)
  Pallas kernels  24.6 us (21%)
  starting transfers between devices  14.4 us (12%)
  other arithmetic  5.68 us (5%)
  between operations  1.41 us (1%)
    all_to_all x1, blocking collectives, exchange(): return lax.all_to_all(data, axes, split_axis=0, concat_axis=0, tiled=True)  34.7 us
    all_to_all x2, waiting for transfers between devices, exchange(): return lax.all_to_all(data, axes, split_axis=0, concat_axis=0, tiled=True)  30.5 us
    pallas_call x1, Pallas kernels, body(): pl.pallas_call(orthogonalize, out_shape=pltpu.HBM((ranks * rows, width),...  13.7 us
    all_to_all x2, starting transfers between devices, exchange(): return lax.all_to_all(data, axes, split_axis=0, concat_axis=0, tiled=True)  12.5 us
    pallas_call x1, Pallas kernels, body(): pl.pallas_call(gather_old, out_shape=(pltpu.HBM((ranks, half, width), bf1...  4.44 us
    convert_element_type x1, other arithmetic, body(): new = new.astype(bf16).reshape(weight.shape)  2.83 us
    pallas_call x1, Pallas kernels, body(): pl.pallas_call(combine, out_shape=(pltpu.HBM((ranks, 2 * planes, lanes, 1...  2.79 us
    ppermute x1, waiting for transfers between devices, body(): theirs = lax.ppermute(theirs, 'core', swap)  2.36 us
  transfers between devices with their start and end apart: 6, of which 5 were waited for; matrix products, arithmetic and copies ran while one was open for 5% of the time, Pallas kernels for 4%

profile of v6, /device:TPU:1, one launch (start us, length us, event | category | flops | bytes accessed | tf_op | source)
XLA Modules:
  0.0 115.5 jit_solution(7858802853084465264)
XLA Ops:
  0.6 2.3 %narrow.1 = bf16[16,128,512]{2,1,0:T(8,128)(2,1)S(1)} custom-call(f32[16,128,512]{2,1,0:T(8,128)} %far_ref.1), custom_call_target="tpu_custom_call" | custom-call | tf_op jit(solution)/shard_map/narrow/pallas_call | solution.py:211
  2.9 34.7 %all_to_all.15 = bf16[16,128,512]{2,1,0:T(8,128)(2,1)S(1)} all-to-all(bf16[16,128,512]{2,1,0:T(8,128)(2,1)S(1)} %narrow.1), channel_id=1, replica_groups=mesh['y'=4,'core'=2,'z'=4,'x'=4] {'x','z'}, dimensions={0} | all-to-all | bytes 4194304 | tf_op jit(solution)/shard_map/all_to_all | solution.py:209
  37.7 13.7 %orthogonalize.1 = bf16[2048,512]{1,0:T(8,128)(2,1)} custom-call(bf16[2048,512]{1,0:T(8,128)(2,1)S(1)} %bitcast.18), custom_call_target="tpu_custom_call" | custom-call | tf_op jit(solution)/shard_map/orthogonalize/pallas_call | solution.py:245
  51.4 0.0 copy-start.1
  51.4 6.6 %all-to-all-start.1 = ((bf16[32,64,512]{2,1,0:T(8,128)(2,1)}), bf16[32,64,512]{2,1,0:T(8,128)(2,1)S(1)}, u32[]{:S(2)}, u32[]{:S(2)}) async-start(bf16[32,64,512]{2,1,0:T(8,128)(2,1)} %bitcast.21), calls=%async_computation.1 | async-start | bytes 4194304 | tf_op jit(solution)/shard_map/all_to_all | solution.py:209
  58.0 4.4 %gather_old.1 = (bf16[16,64,512]{2,1,0:T(8,128)(2,1)}, bf16[16,64,512]{2,1,0:T(8,128)(2,1)}, s32[2,16]{1,0:T(2,128)S(1)}) custom-call(s32[16]{0:T(128)S(1)} %bitcast.20, s32[1]{0:T(128)} %bitcast.6.core_ref, bf16[16,128,512]{2,1,0:T(8,128)(2,1)} %weight_ref.1), custom_call_target="tpu_custom_call" | custom-call | tf_op jit(solution)/shard_map/gather_old/pallas_call | solution.py:223
  62.5 0.4 collective-permute-start.1
  62.8 0.2 collective-permute-start
  63.0 2.4 %collective-permute-done.1 = bf16[16,64,512]{2,1,0:T(8,128)(2,1)S(1)} collective-permute-done((bf16[16,64,512]{2,1,0:T(8,128)(2,1)}, bf16[16,64,512]{2,1,0:T(8,128)(2,1)S(1)}, u32[]{:S(2)}, u32[]{:S(2)}) %collective-permute-start.1) | collective-permute-done | bytes 1048608 | tf_op jit(solution)/shard_map/ppermute | solution.py:241
  65.4 1.5 %add_convert_fusion.old_ref = bf16[16,64,512]{2,1,0:T(8,128)(2,1)S(1)} fusion(bf16[16,64,512]{2,1,0:T(8,128)(2,1)S(1)} %collective-permute-done.1, bf16[16,64,512]{2,1,0:T(8,128)(2,1)} %get-tuple-element.11), kind=kLoop, calls=%fused_computation.2 | loop fusion | flops 2097152 | bytes 3145728 | tf_op jit(solution)/shard_map/convert_element_type | solution.py:243
  67.0 19.3 %all-to-all-done.1 = bf16[32,64,512]{2,1,0:T(8,128)(2,1)S(1)} async-done(((bf16[32,64,512]{2,1,0:T(8,128)(2,1)}), bf16[32,64,512]{2,1,0:T(8,128)(2,1)S(1)}, u32[]{:S(2)}, u32[]{:S(2)}) %all-to-all-start.1) | async-done | bytes 2097184 | tf_op jit(solution)/shard_map/all_to_all | solution.py:209
  86.3 2.8 %combine.1 = (bf16[16,8,32,128]{3,2,1,0:T(8,128)(2,1)}, bf16[8,64,512]{2,1,0:T(8,128)(2,1)}, bf16[8,64,512]{2,1,0:T(8,128)(2,1)}) custom-call(s32[2,16]{1,0:T(2,128)S(1)} %get-tuple-element.10.table_ref, s32[2,16]{1,0:T(2,128)S(1)} %collective-permute-done.pair_ref, s32[1]{0:T(128)} %bitcast.6.core_ref, bf16[16,64,512]{2,1,0:T(8,128)(2,1)S(1)} %add_convert_fusion.old_ref, ...), custom_call_target="tpu_custom_call" | custom-call | tf_op jit(solution)/shard_map/combine/pallas_call | solution.py:263
  89.1 5.9 %all-to-all-start.2 = ((bf16[128,32,128]{2,1,0:T(8,128)(2,1)}), bf16[128,32,128]{2,1,0:T(8,128)(2,1)S(1)}, u32[]{:S(2)}, u32[]{:S(2)}) async-start(bf16[128,32,128]{2,1,0:T(8,128)(2,1)} %bitcast.22), calls=%async_computation.2 | async-start | bytes 2097152 | tf_op jit(solution)/shard_map/all_to_all | solution.py:209
  95.0 1.1 collective-permute-start.2
  96.2 0.1 collective-permute-start.3
  96.3 0.1 broadcast_in_dim.38
  96.3 0.1 broadcast_in_dim.39
  97.1 0.1 dynamic-slice_bitcast_fusion
  97.2 0.9 collective-permute-done.2
  98.0 0.7 collective-permute-done.3
  98.8 1.3 %pad_maximum_fusion = bf16[16,64,512]{2,1,0:T(8,128)(2,1)S(1)} fusion(bf16[8,64,512]{2,1,0:T(8,128)(2,1)} %collective-permute-done.3, bf16[8,64,512]{2,1,0:T(8,128)(2,1)} %collective-permute-done.2), kind=kLoop, calls=%fused_computation.3 | loop fusion | flops 524288 | bytes 2097152 | tf_op jit(solution)/shard_map/concatenate | solution.py:288
  100.1 2.8 %subtract_convert_fusion = bf16[16,128,512]{2,1,0:T(8,128)(2,1)} fusion(bf16[16,128,512]{2,1,0:T(8,128)(2,1)S(1)} %copy-done.2, pred[128]{0:T(512)(128)(4,1)S(1)} %broadcast_in_dim.39, bf16[16,64,512]{2,1,0:T(8,128)(2,1)S(1)} %pad_maximum_fusion, bf16[16,64,512]{2,1,0:T(8,128)(2,1)S(1)} %dynamic-slice_bitcast_fusion), kind=kLoop, calls=%fused_computation | loop fusion | flops 6291456 | bytes 6291584 | tf_op jit(solution)/shard_map/convert_element_type | solution.py:293
  102.9 11.1 %all-to-all-done.2 = bf16[128,32,128]{2,1,0:T(8,128)(2,1)S(1)} async-done(((bf16[128,32,128]{2,1,0:T(8,128)(2,1)}), bf16[128,32,128]{2,1,0:T(8,128)(2,1)S(1)}, u32[]{:S(2)}, u32[]{:S(2)}) %all-to-all-start.2) | async-done | bytes 1048608 | tf_op jit(solution)/shard_map/all_to_all | solution.py:209
  114.1 1.4 %project.1 = bf16[64,384]{1,0:T(8,128)(2,1)} custom-call(s32[1]{0:T(128)S(6)} %copy.7.count_ref, s32[1]{0:T(128)} %bitcast.6.core_ref, bf16[384,2048]{1,0:T(8,128)(2,1)S(1)} %copy-done, bf16[16,4,2,32,128]{4,3,2,1,0:T(8,128)(2,1)S(1)} %bitcast.19), custom_call_target="tpu_custom_call" | custom-call | tf_op jit(solution)/shard_map/project/pallas_call | solution.py:295
  (7 shorter events, 0.0 us)
Async XLA Ops:
  51.4 6.6 %copy-start.1 = (s32[16,1]{0,1:T(1,128)S(1)}, s32[16,1]{0,1:T(1,128)}, u32[]{:S(2)}) copy-start(s32[16,1]{0,1:T(1,128)} %param.7) | copy-start | bytes 196
  51.4 34.9 %all-to-all-start.1 = ((bf16[32,64,512]{2,1,0:T(8,128)(2,1)}), bf16[32,64,512]{2,1,0:T(8,128)(2,1)S(1)}, u32[]{:S(2)}, u32[]{:S(2)}) async-start(bf16[32,64,512]{2,1,0:T(8,128)(2,1)} %bitcast.21), calls=%async_computation.1 | async-start | bytes 4194304 | tf_op jit(solution)/shard_map/all_to_all | solution.py:209
  62.5 3.0 %collective-permute-start.1 = (bf16[16,64,512]{2,1,0:T(8,128)(2,1)}, bf16[16,64,512]{2,1,0:T(8,128)(2,1)S(1)}, u32[]{:S(2)}, u32[]{:S(2)}) collective-permute-start(bf16[16,64,512]{2,1,0:T(8,128)(2,1)} %get-tuple-element.12), channel_id=1, source_target_pairs={{0,16},{16,0},{1,17},{17,1},{2,18},{18,2},{3,19},{19,3},{4,20},{20... | collective-permute-start | bytes 3145736 | tf_op jit(solution)/shard_map/ppermute | solution.py:241
  62.8 4.1 %collective-permute-start = (s32[2,16]{1,0:T(2,128)S(1)}, s32[2,16]{1,0:T(2,128)S(1)}, u32[]{:S(2)}, u32[]{:S(2)}) collective-permute-start(s32[2,16]{1,0:T(2,128)S(1)} %get-tuple-element.10.table_ref), channel_id=1, source_target_pairs={{0,16},{16,0},{1,17},{17,1},{2,18},{18,2},{3,19},{19,3},{4,20},{20... | collective-permute-start | bytes 392 | tf_op jit(solution)/shard_map/ppermute | solution.py:242
  89.1 25.0 %all-to-all-start.2 = ((bf16[128,32,128]{2,1,0:T(8,128)(2,1)}), bf16[128,32,128]{2,1,0:T(8,128)(2,1)S(1)}, u32[]{:S(2)}, u32[]{:S(2)}) async-start(bf16[128,32,128]{2,1,0:T(8,128)(2,1)} %bitcast.22), calls=%async_computation.2 | async-start | bytes 2097152 | tf_op jit(solution)/shard_map/all_to_all | solution.py:209
  95.0 3.0 %collective-permute-start.2 = (bf16[8,64,512]{2,1,0:T(8,128)(2,1)}, bf16[8,64,512]{2,1,0:T(8,128)(2,1)}, u32[]{:S(2)}, u32[]{:S(2)}) collective-permute-start(bf16[8,64,512]{2,1,0:T(8,128)(2,1)} %get-tuple-element.13), channel_id=1, source_target_pairs={{0,16},{16,0},{1,17},{17,1},{2,18},{18,2},{3,19},{19,3},{4,20},{20... | collective-permute-start | bytes 1572872 | tf_op jit(solution)/shard_map/ppermute | solution.py:288
  96.2 2.6 %collective-permute-start.3 = (bf16[8,64,512]{2,1,0:T(8,128)(2,1)}, bf16[8,64,512]{2,1,0:T(8,128)(2,1)}, u32[]{:S(2)}, u32[]{:S(2)}) collective-permute-start(bf16[8,64,512]{2,1,0:T(8,128)(2,1)} %get-tuple-element.14), channel_id=1, source_target_pairs={{0,16},{16,0},{1,17},{17,1},{2,18},{18,2},{3,19},{19,3},{4,20},{20... | collective-permute-start | bytes 1572872 | tf_op jit(solution)/shard_map/ppermute | solution.py:288
  97.1 3.0 %copy-start.2 = (bf16[16,128,512]{2,1,0:T(8,128)(2,1)S(1)}, bf16[16,128,512]{2,1,0:T(8,128)(2,1)}, u32[]{:S(2)}) copy-start(bf16[16,128,512]{2,1,0:T(8,128)(2,1)} %weight_ref.1) | copy-start | bytes 6291460
  100.1 14.0 %copy-start = (bf16[384,2048]{1,0:T(8,128)(2,1)S(1)}, bf16[384,2048]{1,0:T(8,128)(2,1)}, u32[]{:S(2)}) copy-start(bf16[384,2048]{1,0:T(8,128)(2,1)} %tokens_ref.1) | copy-start | bytes 4718596

commit v7 on v6

--- a/solution.py
+++ b/solution.py
@@ -213,7 +213,7 @@
         out_shape=jax.ShapeDtypeStruct(grad.shape, bf16),
         in_specs=[hbm],
         out_specs=vmem,
-        scratch_shapes=[pltpu.VMEM(grad.shape, f32), pltpu.SemaphoreType.DMA((16,))],
+        scratch_shapes=[pltpu.VMEM(grad.shape, f32), pltpu.SemaphoreType.DMA((8,))],
         compiler_params=params,
         name="narrow",
     )(pltpu.with_memory_space_constraint(grad, pltpu.HBM))

time: 116 us -> 116 us (level)
  no operation moved by 1% of the time
where the time goes in v7:
time: 116 us; the launch traced here: 115 us
  blocking collectives  34.7 us (30%)
  waiting for transfers between devices  34.5 us (30%)
  Pallas kernels  24.5 us (21%)
  starting transfers between devices  14.3 us (12%)
  other arithmetic  5.68 us (5%)
  between operations  1.41 us (1%)
    all_to_all x1, blocking collectives, exchange(): return lax.all_to_all(data, axes, split_axis=0, concat_axis=0, tiled=True)  34.7 us
    all_to_all x2, waiting for transfers between devices, exchange(): return lax.all_to_all(data, axes, split_axis=0, concat_axis=0, tiled=True)  30.5 us
    pallas_call x1, Pallas kernels, body(): pl.pallas_call(orthogonalize, out_shape=pltpu.HBM((ranks * rows, width),...  13.7 us
    all_to_all x2, starting transfers between devices, exchange(): return lax.all_to_all(data, axes, split_axis=0, concat_axis=0, tiled=True)  12.5 us
    pallas_call x1, Pallas kernels, body(): pl.pallas_call(gather_old, out_shape=(pltpu.HBM((ranks, half, width), bf1...  4.44 us
    convert_element_type x1, other arithmetic, body(): new = new.astype(bf16).reshape(weight.shape)  2.83 us
    pallas_call x1, Pallas kernels, body(): pl.pallas_call(combine, out_shape=(pltpu.HBM((ranks, 2 * planes, lanes, 1...  2.79 us
    ppermute x1, waiting for transfers between devices, body(): theirs = lax.ppermute(theirs, 'core', swap)  2.36 us
  transfers between devices with their start and end apart: 6, of which 5 were waited for; matrix products, arithmetic and copies ran while one was open for 5% of the time, Pallas kernels for 4%

profile of v7, /device:TPU:1, one launch (start us, length us, event | category | flops | bytes accessed | tf_op | source)
XLA Modules:
  0.0 115.4 jit_solution(8172491438257560827)
XLA Ops:
  0.6 2.2 %narrow.1 = bf16[16,128,512]{2,1,0:T(8,128)(2,1)S(1)} custom-call(f32[16,128,512]{2,1,0:T(8,128)} %far_ref.1), custom_call_target="tpu_custom_call" | custom-call | tf_op jit(solution)/shard_map/narrow/pallas_call | solution.py:211
  2.9 34.7 %all_to_all.15 = bf16[16,128,512]{2,1,0:T(8,128)(2,1)S(1)} all-to-all(bf16[16,128,512]{2,1,0:T(8,128)(2,1)S(1)} %narrow.1), channel_id=1, replica_groups=mesh['y'=4,'core'=2,'z'=4,'x'=4] {'x','z'}, dimensions={0} | all-to-all | bytes 4194304 | tf_op jit(solution)/shard_map/all_to_all | solution.py:209
  37.6 13.7 %orthogonalize.1 = bf16[2048,512]{1,0:T(8,128)(2,1)} custom-call(bf16[2048,512]{1,0:T(8,128)(2,1)S(1)} %bitcast.18), custom_call_target="tpu_custom_call" | custom-call | tf_op jit(solution)/shard_map/orthogonalize/pallas_call | solution.py:245
  51.3 0.0 copy-start.1
  51.3 6.6 %all-to-all-start.1 = ((bf16[32,64,512]{2,1,0:T(8,128)(2,1)}), bf16[32,64,512]{2,1,0:T(8,128)(2,1)S(1)}, u32[]{:S(2)}, u32[]{:S(2)}) async-start(bf16[32,64,512]{2,1,0:T(8,128)(2,1)} %bitcast.21), calls=%async_computation.1 | async-start | bytes 4194304 | tf_op jit(solution)/shard_map/all_to_all | solution.py:209
  58.0 4.4 %gather_old.1 = (bf16[16,64,512]{2,1,0:T(8,128)(2,1)}, bf16[16,64,512]{2,1,0:T(8,128)(2,1)}, s32[2,16]{1,0:T(2,128)S(1)}) custom-call(s32[16]{0:T(128)S(1)} %bitcast.20, s32[1]{0:T(128)} %bitcast.6.core_ref, bf16[16,128,512]{2,1,0:T(8,128)(2,1)} %weight_ref.1), custom_call_target="tpu_custom_call" | custom-call | tf_op jit(solution)/shard_map/gather_old/pallas_call | solution.py:223
  62.4 0.4 collective-permute-start.1
  62.8 0.2 collective-permute-start
  63.0 2.4 %collective-permute-done.1 = bf16[16,64,512]{2,1,0:T(8,128)(2,1)S(1)} collective-permute-done((bf16[16,64,512]{2,1,0:T(8,128)(2,1)}, bf16[16,64,512]{2,1,0:T(8,128)(2,1)S(1)}, u32[]{:S(2)}, u32[]{:S(2)}) %collective-permute-start.1) | collective-permute-done | bytes 1048608 | tf_op jit(solution)/shard_map/ppermute | solution.py:241
  65.4 1.5 %add_convert_fusion.old_ref = bf16[16,64,512]{2,1,0:T(8,128)(2,1)S(1)} fusion(bf16[16,64,512]{2,1,0:T(8,128)(2,1)S(1)} %collective-permute-done.1, bf16[16,64,512]{2,1,0:T(8,128)(2,1)} %get-tuple-element.11), kind=kLoop, calls=%fused_computation.2 | loop fusion | flops 2097152 | bytes 3145728 | tf_op jit(solution)/shard_map/convert_element_type | solution.py:243
  66.9 19.3 %all-to-all-done.1 = bf16[32,64,512]{2,1,0:T(8,128)(2,1)S(1)} async-done(((bf16[32,64,512]{2,1,0:T(8,128)(2,1)}), bf16[32,64,512]{2,1,0:T(8,128)(2,1)S(1)}, u32[]{:S(2)}, u32[]{:S(2)}) %all-to-all-start.1) | async-done | bytes 2097184 | tf_op jit(solution)/shard_map/all_to_all | solution.py:209
  86.3 2.8 %combine.1 = (bf16[16,8,32,128]{3,2,1,0:T(8,128)(2,1)}, bf16[8,64,512]{2,1,0:T(8,128)(2,1)}, bf16[8,64,512]{2,1,0:T(8,128)(2,1)}) custom-call(s32[2,16]{1,0:T(2,128)S(1)} %get-tuple-element.10.table_ref, s32[2,16]{1,0:T(2,128)S(1)} %collective-permute-done.pair_ref, s32[1]{0:T(128)} %bitcast.6.core_ref, bf16[16,64,512]{2,1,0:T(8,128)(2,1)S(1)} %add_convert_fusion.old_ref, ...), custom_call_target="tpu_custom_call" | custom-call | tf_op jit(solution)/shard_map/combine/pallas_call | solution.py:263
  89.1 5.9 %all-to-all-start.2 = ((bf16[128,32,128]{2,1,0:T(8,128)(2,1)}), bf16[128,32,128]{2,1,0:T(8,128)(2,1)S(1)}, u32[]{:S(2)}, u32[]{:S(2)}) async-start(bf16[128,32,128]{2,1,0:T(8,128)(2,1)} %bitcast.22), calls=%async_computation.2 | async-start | bytes 2097152 | tf_op jit(solution)/shard_map/all_to_all | solution.py:209
  95.0 1.1 collective-permute-start.2
  96.1 0.1 collective-permute-start.3
  96.2 0.1 broadcast_in_dim.38
  96.3 0.1 broadcast_in_dim.39
  97.0 0.1 dynamic-slice_bitcast_fusion
  97.1 0.9 collective-permute-done.2
  98.0 0.7 collective-permute-done.3
  98.7 1.3 %pad_maximum_fusion = bf16[16,64,512]{2,1,0:T(8,128)(2,1)S(1)} fusion(bf16[8,64,512]{2,1,0:T(8,128)(2,1)} %collective-permute-done.3, bf16[8,64,512]{2,1,0:T(8,128)(2,1)} %collective-permute-done.2), kind=kLoop, calls=%fused_computation.3 | loop fusion | flops 524288 | bytes 2097152 | tf_op jit(solution)/shard_map/concatenate | solution.py:288
  100.1 2.8 %subtract_convert_fusion = bf16[16,128,512]{2,1,0:T(8,128)(2,1)} fusion(bf16[16,128,512]{2,1,0:T(8,128)(2,1)S(1)} %copy-done.2, pred[128]{0:T(512)(128)(4,1)S(1)} %broadcast_in_dim.39, bf16[16,64,512]{2,1,0:T(8,128)(2,1)S(1)} %pad_maximum_fusion, bf16[16,64,512]{2,1,0:T(8,128)(2,1)S(1)} %dynamic-slice_bitcast_fusion), kind=kLoop, calls=%fused_computation | loop fusion | flops 6291456 | bytes 6291584 | tf_op jit(solution)/shard_map/convert_element_type | solution.py:293
  102.9 11.1 %all-to-all-done.2 = bf16[128,32,128]{2,1,0:T(8,128)(2,1)S(1)} async-done(((bf16[128,32,128]{2,1,0:T(8,128)(2,1)}), bf16[128,32,128]{2,1,0:T(8,128)(2,1)S(1)}, u32[]{:S(2)}, u32[]{:S(2)}) %all-to-all-start.2) | async-done | bytes 1048608 | tf_op jit(solution)/shard_map/all_to_all | solution.py:209
  114.0 1.4 %project.1 = bf16[64,384]{1,0:T(8,128)(2,1)} custom-call(s32[1]{0:T(128)S(6)} %copy.7.count_ref, s32[1]{0:T(128)} %bitcast.6.core_ref, bf16[384,2048]{1,0:T(8,128)(2,1)S(1)} %copy-done, bf16[16,4,2,32,128]{4,3,2,1,0:T(8,128)(2,1)S(1)} %bitcast.19), custom_call_target="tpu_custom_call" | custom-call | tf_op jit(solution)/shard_map/project/pallas_call | solution.py:295
  (7 shorter events, 0.0 us)
Async XLA Ops:
  51.3 6.6 %copy-start.1 = (s32[16,1]{0,1:T(1,128)S(1)}, s32[16,1]{0,1:T(1,128)}, u32[]{:S(2)}) copy-start(s32[16,1]{0,1:T(1,128)} %param.7) | copy-start | bytes 196
  51.3 34.9 %all-to-all-start.1 = ((bf16[32,64,512]{2,1,0:T(8,128)(2,1)}), bf16[32,64,512]{2,1,0:T(8,128)(2,1)S(1)}, u32[]{:S(2)}, u32[]{:S(2)}) async-start(bf16[32,64,512]{2,1,0:T(8,128)(2,1)} %bitcast.21), calls=%async_computation.1 | async-start | bytes 4194304 | tf_op jit(solution)/shard_map/all_to_all | solution.py:209
  62.4 3.0 %collective-permute-start.1 = (bf16[16,64,512]{2,1,0:T(8,128)(2,1)}, bf16[16,64,512]{2,1,0:T(8,128)(2,1)S(1)}, u32[]{:S(2)}, u32[]{:S(2)}) collective-permute-start(bf16[16,64,512]{2,1,0:T(8,128)(2,1)} %get-tuple-element.12), channel_id=1, source_target_pairs={{0,16},{16,0},{1,17},{17,1},{2,18},{18,2},{3,19},{19,3},{4,20},{20... | collective-permute-start | bytes 3145736 | tf_op jit(solution)/shard_map/ppermute | solution.py:241
  62.8 4.1 %collective-permute-start = (s32[2,16]{1,0:T(2,128)S(1)}, s32[2,16]{1,0:T(2,128)S(1)}, u32[]{:S(2)}, u32[]{:S(2)}) collective-permute-start(s32[2,16]{1,0:T(2,128)S(1)} %get-tuple-element.10.table_ref), channel_id=1, source_target_pairs={{0,16},{16,0},{1,17},{17,1},{2,18},{18,2},{3,19},{19,3},{4,20},{20... | collective-permute-start | bytes 392 | tf_op jit(solution)/shard_map/ppermute | solution.py:242
  89.1 25.0 %all-to-all-start.2 = ((bf16[128,32,128]{2,1,0:T(8,128)(2,1)}), bf16[128,32,128]{2,1,0:T(8,128)(2,1)S(1)}, u32[]{:S(2)}, u32[]{:S(2)}) async-start(bf16[128,32,128]{2,1,0:T(8,128)(2,1)} %bitcast.22), calls=%async_computation.2 | async-start | bytes 2097152 | tf_op jit(solution)/shard_map/all_to_all | solution.py:209
  95.0 3.0 %collective-permute-start.2 = (bf16[8,64,512]{2,1,0:T(8,128)(2,1)}, bf16[8,64,512]{2,1,0:T(8,128)(2,1)}, u32[]{:S(2)}, u32[]{:S(2)}) collective-permute-start(bf16[8,64,512]{2,1,0:T(8,128)(2,1)} %get-tuple-element.13), channel_id=1, source_target_pairs={{0,16},{16,0},{1,17},{17,1},{2,18},{18,2},{3,19},{19,3},{4,20},{20... | collective-permute-start | bytes 1572872 | tf_op jit(solution)/shard_map/ppermute | solution.py:288
  96.1 2.6 %collective-permute-start.3 = (bf16[8,64,512]{2,1,0:T(8,128)(2,1)}, bf16[8,64,512]{2,1,0:T(8,128)(2,1)}, u32[]{:S(2)}, u32[]{:S(2)}) collective-permute-start(bf16[8,64,512]{2,1,0:T(8,128)(2,1)} %get-tuple-element.14), channel_id=1, source_target_pairs={{0,16},{16,0},{1,17},{17,1},{2,18},{18,2},{3,19},{19,3},{4,20},{20... | collective-permute-start | bytes 1572872 | tf_op jit(solution)/shard_map/ppermute | solution.py:288
  97.0 3.0 %copy-start.2 = (bf16[16,128,512]{2,1,0:T(8,128)(2,1)S(1)}, bf16[16,128,512]{2,1,0:T(8,128)(2,1)}, u32[]{:S(2)}) copy-start(bf16[16,128,512]{2,1,0:T(8,128)(2,1)} %weight_ref.1) | copy-start | bytes 6291460
  100.0 14.0 %copy-start = (bf16[384,2048]{1,0:T(8,128)(2,1)S(1)}, bf16[384,2048]{1,0:T(8,128)(2,1)}, u32[]{:S(2)}) copy-start(bf16[384,2048]{1,0:T(8,128)(2,1)} %tokens_ref.1) | copy-start | bytes 4718596
